TPU v7x, 128 devices: a whole 4x4x4 slice. The times are simulated.
128 devices in a mesh: axial: 8 (over x, core), azim: 16 (over z, y).
Axes of the slice: x: 4, y: 4, z: 4, core: 2. Of those that a mesh axis runs over, the one named last changes fastest.
Arguments:
- cycle_state: float32 [5, 64, 2048, 256], P(None, 'axial', 'azim'), as said below
- core_state: float32 [5, 64, 192, 192], P(None, 'axial', 'azim'), as said below
- core_taps: int32 [768, 4], replicated, may hold values from 0 to 2047, as said below
- core_weights: float32 [768, 4], replicated, may hold values from 0.1 to 1
- cycle_taps: int32 [2048, 4], replicated, may hold values from 0 to 36863, as said below
- cycle_weights: float32 [2048, 4], replicated, may hold values from 0.1 to 1
Outputs:
- cycle_new: float32 [5, 64, 2048, 256], P(None, 'axial', 'azim')
- core_new: float32 [5, 64, 192, 192], P(None, 'axial', 'azim')
Inputs may be any that keep to these rules, and one draw needn't show every extreme that they name: `core_taps`: cycle positions, each within 8 positions (cyclically) of position g * 2048 // 768. `cycle_taps`: flat indices of core cells within three cells of the core's edge. `cycle_state`: density (component 0) lies in 0.5 to 1.5. `core_state`: density (component 0) lies in 0.5 to 1.5.
All inputs are finite; a program needn't handle non-finite values.
Results may differ from a plain program's by a relative error of at most 0.0003.
Values sent between devices are 32-bit elements; how exact they have to be, the bound alone decides.
A program may use at most 128 MiB of HBM per device.

v0:
```python
import math

import jax
import jax.numpy as jnp
from jax import lax
from jax.sharding import PartitionSpec as P

time_step = 0.001
axial_step = 0.004
radial_step = 1.0 / 256.0
core_step = 2.0 / 192.0
inner_radius = 1.0
viscosity = 0.002
gamma_minus = 0.4


def padded_2(block, sides, width):
    for axis, dim in sides:
        count = lax.axis_size(axis)
        forward = [(i, i + 1) for i in range(count - 1)]
        forward.append((count - 1, 0))
        backward = [(target, source) for source, target in forward]
        low = lax.ppermute(
            lax.slice_in_dim(block, block.shape[dim] - width, None, axis=dim), axis, forward
        )
        high = lax.ppermute(lax.slice_in_dim(block, 0, width, axis=dim), axis, backward)
        block = jnp.concatenate([low, block, high], axis=dim)
    return block


def pressure_of(state):
    kinetic = 0.5 * (state[1] * state[1] + state[2] * state[2] + state[3] * state[3]) / state[0]
    return gamma_minus * (state[4] - kinetic)


def fluxes(state, component):
    pressure = pressure_of(state)
    velocity = state[component] / state[0]
    parts = [
        state[component],
        state[1] * velocity,
        state[2] * velocity,
        state[3] * velocity,
        (state[4] + pressure) * velocity,
    ]
    parts[component] = parts[component] + pressure
    return jnp.stack(parts, axis=0)


def angle_of(positions, total):
    return (positions.astype(jnp.float32) + 0.5) * (2.0 * math.pi / total)


def to_cartesian(trace, angles):
    cosine = jnp.cos(angles)
    sine = jnp.sin(angles)
    y_part = trace[3] * cosine - trace[2] * sine
    z_part = trace[3] * sine + trace[2] * cosine
    return jnp.stack([trace[0], trace[1], y_part, z_part, trace[4]], axis=0)


def to_polar(trace, angles):
    cosine = jnp.cos(angles)
    sine = jnp.sin(angles)
    azimuthal = trace[3] * cosine - trace[2] * sine
    radial = trace[2] * cosine + trace[3] * sine
    return jnp.stack([trace[0], trace[1], azimuthal, radial, trace[4]], axis=0)


def normalized(weights):
    return weights / jnp.sum(weights, axis=1, keepdims=True)


def tap_matrix(taps, weights, offset, count):
    sources = jnp.arange(count, dtype=jnp.int32)[:, None]
    local_idx = taps - offset
    matrix = jnp.zeros((count, taps.shape[0]), jnp.float32)
    for which in range(taps.shape[1]):
        hits = sources == local_idx[:, which][None, :]
        matrix = matrix + jnp.where(hits, weights[:, which][None, :], 0.0)
    return matrix


def apply_taps(values, matrix):
    lead = values.shape[:2]
    flat_values = values.reshape(lead[0] * lead[1], values.shape[2])
    result = jnp.dot(
        flat_values, matrix, preferred_element_type=jnp.float32, precision=lax.Precision.HIGHEST
    )
    return result.reshape(lead[0], lead[1], matrix.shape[1])


def radius_full(count):
    return inner_radius + (jnp.arange(count + 2).astype(jnp.float32) - 0.5) * radial_step


def cycle_rhs(padded, inner_ghost, angle_step):
    center = padded[:, 1:-1, 1:-1]
    reflect = jnp.array([1.0, 1.0, 1.0, -1.0, 1.0], jnp.float32)[:, None, None]
    outer_ghost = center[:, :, :, -1] * reflect
    radial_pad = jnp.concatenate([inner_ghost[..., None], center, outer_ghost[..., None]], axis=3)
    radius = radius_full(center.shape[3])
    mid_radius = radius[1:-1]
    arc = angle_step * mid_radius
    axial_flux = fluxes(padded[:, :, 1:-1], 1)
    azim_flux = fluxes(padded[:, 1:-1], 2)
    radial_flux = fluxes(radial_pad, 3)
    divergence = (axial_flux[:, 2:] - axial_flux[:, :-2]) / (2.0 * axial_step)
    divergence = divergence + (azim_flux[:, :, 2:] - azim_flux[:, :, :-2]) / (2.0 * arc)
    divergence = divergence + (
        radius[2:] * radial_flux[..., 2:] - radius[:-2] * radial_flux[..., :-2]
    ) / (2.0 * radial_step * mid_radius)
    laplace = (padded[:, 2:, 1:-1] - 2.0 * center + padded[:, :-2, 1:-1]) / (
        axial_step * axial_step
    )
    laplace = laplace + (padded[:, 1:-1, 2:] - 2.0 * center + padded[:, 1:-1, :-2]) / (arc * arc)
    laplace = laplace + (radial_pad[..., 2:] - 2.0 * center + radial_pad[..., :-2]) / (
        radial_step * radial_step
    )
    pressure = pressure_of(center)
    swirl = -center[2] * center[3] / (center[0] * mid_radius)
    outward = (center[2] * center[2] / center[0] + pressure) / mid_radius
    zero_part = jnp.zeros_like(swirl)
    source = jnp.stack([zero_part, zero_part, swirl, outward, zero_part], axis=0)
    return -divergence + source + viscosity * laplace


def core_rhs(axial_pad, row_pad, left_col, right_col):
    center = axial_pad[:, 1:-1]
    col_pad = jnp.concatenate([left_col[..., None], center, right_col[..., None]], axis=3)
    axial_flux = fluxes(axial_pad, 1)
    row_flux = fluxes(row_pad, 2)
    col_flux = fluxes(col_pad, 3)
    divergence = (axial_flux[:, 2:] - axial_flux[:, :-2]) / (2.0 * axial_step)
    divergence = divergence + (row_flux[:, :, 2:] - row_flux[:, :, :-2]) / (2.0 * core_step)
    divergence = divergence + (col_flux[..., 2:] - col_flux[..., :-2]) / (2.0 * core_step)
    laplace = (axial_pad[:, 2:] - 2.0 * center + axial_pad[:, :-2]) / (axial_step * axial_step)
    laplace = laplace + (row_pad[:, :, 2:] - 2.0 * center + row_pad[:, :, :-2]) / (
        core_step * core_step
    )
    laplace = laplace + (col_pad[..., 2:] - 2.0 * center + col_pad[..., :-2]) / (
        core_step * core_step
    )
    return -divergence + viscosity * laplace


def body(cycle_state, core_state, core_taps, core_weights, cycle_taps, cycle_weights):
    channels, planes, sector, radial_cells = cycle_state.shape
    core_rows = core_state.shape[2]
    core_cells = core_state.shape[3]
    n_azim = lax.axis_size("azim")
    own_index = lax.axis_index("azim")
    positions_all = sector * n_azim
    angle_step = 2.0 * math.pi / positions_all
    angles = angle_of(own_index * sector + jnp.arange(sector, dtype=jnp.int32), positions_all)
    cart_trace = to_cartesian(cycle_state[:, :, :, 0], angles)
    core_norm = normalized(core_weights)
    all_traces = lax.all_gather(cart_trace, "azim", axis=2, tiled=True)
    ghost_matrix = tap_matrix(core_taps, core_norm, 0, positions_all)
    ghosts = apply_taps(all_traces, ghost_matrix)
    flat_core = core_state.reshape(channels, planes, core_rows * core_cells)
    cycle_matrix = tap_matrix(
        cycle_taps,
        normalized(cycle_weights),
        own_index * core_rows * core_cells,
        core_rows * core_cells,
    )
    cycle_share = apply_taps(flat_core, cycle_matrix)
    inner_cart = lax.psum_scatter(cycle_share, "azim", scatter_dimension=2, tiled=True)
    inner_ghost = to_polar(inner_cart, angles)
    core_pad = padded_2(core_state, (("axial", 1), ("azim", 2)), 1)
    lower = jnp.where(
        own_index == 0, ghosts[:, :, 2 * core_cells : 3 * core_cells], core_pad[:, 1:-1, 0, :]
    )
    upper = jnp.where(
        own_index == n_azim - 1,
        ghosts[:, :, 3 * core_cells : 4 * core_cells],
        core_pad[:, 1:-1, -1, :],
    )
    row_pad = jnp.concatenate([lower[:, :, None], core_state, upper[:, :, None]], axis=2)
    left_col = lax.dynamic_slice_in_dim(ghosts, own_index * core_rows, core_rows, 2)
    right_col = lax.dynamic_slice_in_dim(ghosts, core_cells + own_index * core_rows, core_rows, 2)
    axial_pad = core_pad[:, :, 1:-1, :]
    core_new = core_state + time_step * core_rhs(axial_pad, row_pad, left_col, right_col)
    padded = padded_2(cycle_state, (("axial", 1), ("azim", 2)), 1)
    cycle_new = cycle_state + time_step * cycle_rhs(padded, inner_ghost, angle_step)
    return (cycle_new, core_new)


def solution(mesh):
    placed = (P(None, "axial", "azim", None), P(None, "axial", "azim", None), P(), P(), P(), P())
    return jax.shard_map(
        body,
        mesh=mesh,
        in_specs=placed,
        out_specs=(P(None, "axial", "azim", None), P(None, "axial", "azim", None)),
        check_vma=False,
    )
```

profile of v0, /device:TPU:0, one launch (start us, length us, event | category | flops | bytes accessed | tf_op | source)
XLA Modules:
  0.0 209.3 jit_solution(2949370701455173212)
XLA Ops:
  11.0 21.3 %fusion.57 = f32[5,8,2048]{2,1,0:T(8,128)} fusion(f32[40,2304]{1,0:T(8,128)S(1)} %reshape_reshape.3, f32[2048]{0:T(1024)S(1)} %bitcast.69, s32[2048]{0:T(1024)S(1)} %bitcast.73, f32[2048]{0:T(1024)S(1)} %bitcast.70, s32[2048]{0:T(1024)S(1)} %bitcast.74, f32[2048]{0:T(1024)S(1)} %bitcast.71, s32[2048]{0:T(1024)S(1)} %bitcast.75, f32[2048]{0:T(1024)S(1)} %bitcast.68, ...), kind=kOutput, calls=%fused_computation.78 | convolution fusion | flops 2316828672 | bytes 761856 | tf_op jit(solution)/shard_map/dot_general | solution.py:87
  32.3 2.5 %fusion.92 = (f32[5,1,128,256]{3,2,1,0:T(8,128)}, f32[5,1,128,256]{3,2,1,0:T(8,128)}) fusion(f32[5,8,128,256]{3,2,1,0:T(8,128)} %param.7), kind=kLoop, calls=%fused_computation.210 | loop fusion | bytes 2621440 | tf_op jit(solution)/shard_map/slice | solution.py:26
  34.8 3.0 %collective-permute-start.1 = (f32[5,1,128,256]{3,2,1,0:T(8,128)}, f32[5,1,128,256]{3,2,1,0:T(8,128)S(1)}, u32[]{:S(2)}, u32[]{:S(2)}) collective-permute-start(f32[5,1,128,256]{3,2,1,0:T(8,128)} %get-tuple-element.49), channel_id=1, source_target_pairs={{16,0},{32,16},{48,32},{64,48},{80,64},{96,80},{112,96},{0,112},{1... | collective-permute-start | bytes 1966088 | tf_op jit(solution)/shard_map/ppermute | solution.py:26
  38.3 2.9 %fusion.91 = (f32[1,8,128,1]{3,2,1,0:T(8,128)S(1)}, f32[1,8,128,1]{3,2,1,0:T(8,128)}, f32[1,8,128,1]{3,2,1,0:T(8,128)}, f32[1,8,128,1]{3,2,1,0:T(8,128)S(1)}, f32[1,8,128,1]{3,2,1,0:T(8,128)}) fusion(f32[5,8,128,256]{3,2,1,0:T(8,128)} %param.7), kind=kLoop, calls=%fused_computation.209 | loop fusion | bytes 40960 | tf_op jit(solution)/shard_map/slice | solution.py:59
  45.1 4.0 %slice_multiply_fusion.2 = f32[5,8,128,1]{3,2,1,0:T(8,128)} fusion(f32[5,8,128,256]{3,2,1,0:T(8,128)} %param.7, f32[5]{0:T(128)S(1)} %copy-done.26), kind=kLoop, calls=%fused_computation.77 | loop fusion | flops 5120 | bytes 40980 | tf_op jit(solution)/shard_map/mul | solution.py:100
  49.2 4.4 %multiply_divide_fusion = (f32[1,8,128,256]{3,2,1,0:T(8,128)}, f32[1,8,128,256]{3,2,1,0:T(8,128)}) fusion(f32[5,8,128,256]{3,2,1,0:T(8,128)} %param.7, f32[256]{0:T(256)S(1)} %get-tuple-element.75), kind=kLoop, calls=%fused_computation.105 | loop fusion | flops 4194304 | bytes 7341056 | tf_op jit(solution)/shard_map/div | solution.py:121
  55.6 6.6 %collective-permute-start.7 = (f32[5,10,1,192]{3,1,0,2:T(8,128)}, f32[5,10,1,192]{3,1,0,2:T(8,128)}, u32[]{:S(2)}, u32[]{:S(2)}) collective-permute-start(f32[5,10,1,192]{3,1,0,2:T(8,128)} %get-tuple-element.51), channel_id=1, source_target_pairs={{1,0},{2,1},{3,2},{4,3},{5,4},{6,5},{7,6},{8,7},{9,8},{10,9},{11,1... | collective-permute-start | bytes 115208 | tf_op jit(solution)/shard_map/ppermute | solution.py:26
  62.8 3.9 %constant_dynamic-update-slice_fusion.1 = f32[5,10,128,256]{3,2,1,0:T(8,128)S(1)} fusion(f32[5,10,128,256]{3,2,1,0:T(8,128)S(1)} %constant_dynamic-update-slice_fusion.2, f32[5,8,128,256]{3,2,1,0:T(8,128)} %param.7), kind=kLoop, calls=%fused_computation.163 | loop fusion | bytes 10485760
  67.7 1.9 copy-done
  70.8 36.8 %reduce-scatter.2.cloned.1.call-done = f32[5,8,128]{2,1,0:T(8,128)} async-done(((f32[5,8,2048]{2,1,0:T(8,128)}), f32[5,8,128]{2,1,0:T(8,128)}) %reduce-scatter.2.cloned.1.call-update) | async-done | bytes 20496 | tf_op jit(solution)/shard_map/reduce_scatter | solution.py:169
  109.8 1.3 collective-permute-start.2
  111.0 4.2 %collective-permute-start.3 = (f32[5,10,1,256]{3,2,1,0:T(1,128)}, f32[5,10,1,256]{3,2,1,0:T(1,128)S(1)}, u32[]{:S(2)}, u32[]{:S(2)}) collective-permute-start(f32[5,10,1,256]{3,2,1,0:T(1,128)} %get-tuple-element.40), channel_id=1, source_target_pairs={{1,0},{2,1},{3,2},{4,3},{5,4},{6,5},{7,6},{8,7},{9,8},{10,9},{11,1... | collective-permute-start | bytes 153608 | tf_op jit(solution)/shard_map/ppermute | solution.py:26
  115.2 5.7 %pad_maximum_fusion = f32[5,8,128,258]{3,2,1,0:T(8,128)S(1)} fusion(f32[5,8,128,1]{3,2,1,0:T(8,128)} %slice_multiply_fusion.2, f32[5,8,128,256]{3,2,1,0:T(8,128)} %param.7, f32[5,8,128,1]{3,2,1,0:T(8,128)S(1)} %copy.31), kind=kLoop, calls=%fused_computation.21 | loop fusion | flops 2641920 | bytes 10567680 | tf_op jit(solution)/shard_map/concatenate | solution.py:101
  121.5 3.1 %copy-done.1 = f32[5,8,128,258]{3,2,1,0:T(8,128)} copy-done((f32[5,8,128,258]{3,2,1,0:T(8,128)}, f32[5,8,128,258]{3,2,1,0:T(8,128)S(1)}, u32[]{:S(2)}) %copy-start.1) | copy-done | bytes 5283864
  124.6 1.8 add_dynamic-update-slice_fusion
  127.8 2.7 %add_dynamic-update-slice_fusion.1 = (f32[5,10,128,256]{3,2,1,0:T(8,128)}, f32[1,10,128,256]{3,2,1,0:T(8,128)S(1)}, f32[1,10,128,256]{3,2,1,0:T(8,128)}) fusion(f32[5,10,128,256]{3,2,1,0:T(8,128)} %slice_dynamic-update-slice_fusion.1, f32[5,10,128,256]{3,2,1,0:T(8,128)S(1)} %bitcast.65), kind=kLoop, calls=%fused_computation.88 | loop fusion | flops 3932160 | bytes 10485760
  131.7 1.5 multiply_dynamic-update-slice_fusion.5
  134.4 22.2 %all_gather.3 = f32[5,8,2048]{2,1,0:T(8,128)S(1)} all-gather(f32[5,8,128]{2,1,0:T(8,128)S(1)} %constant_dynamic-update-slice_fusion.4), channel_id=1, replica_groups=mesh['axial'=8,'azim'=16] {'azim'}, dimensions={2}, use_global_device_ids=true | all-gather | bytes 348160 | tf_op jit(solution)/shard_map/all_gather | solution.py:158
  156.7 6.7 %fusion.17 = f32[5,8,768]{2,1,0:T(8,128)S(1)} fusion(f32[5,8,2048]{2,1,0:T(8,128)S(1)} %all_gather.3, f32[768]{0:T(1024)S(1)} %get-tuple-element.11, s32[768]{0:T(1024)S(1)} %get-tuple-element.8, f32[768]{0:T(1024)S(1)} %get-tuple-element.12, s32[768]{0:T(1024)S(1)} %get-tuple-element.9, f32[768]{0:T(1024)S(1)} %get-tuple-element.13, ...), kind=kOutput, calls=%fused_computation.22 | convolution fusion | flops 772276224 | bytes 475136 | tf_op jit(solution)/shard_map/dot_general | solution.py:87
  164.8 1.3 fusion.81
  166.4 3.0 %multiply_dynamic-update-slice_fusion = f32[5,8,128,258]{3,2,1,0:T(8,128)} fusion(f32[5,8,128,258]{3,2,1,0:T(8,128)} %copy-done.10, f32[1,8,128,258]{3,2,1,0:T(8,128)S(1)} %copy-done.3, f32[1,8,128,258]{3,2,1,0:T(8,128)S(1)} %copy-done.11, f32[5,8,128,258]{3,2,1,0:T(8,128)} %copy-done.1), kind=kLoop, calls=%fused_computation.79 | loop fusion | flops 528384 | bytes 5259264 | tf_op jit(solution)/shard_map/stack | solution.py:47
  169.4 1.4 multiply_dynamic-update-slice_fusion.3
  174.5 2.4 %copy-done.4 = f32[5,8,130,256]{3,2,1,0:T(8,128)} copy-done((f32[5,8,130,256]{3,2,1,0:T(8,128)}, f32[5,8,130,256]{3,2,1,0:T(8,128)S(1)}, u32[]{:S(2)}) %copy-start.4) | copy-done | bytes 5324824
  176.9 25.6 %fusion.32 = f32[5,8,128,256]{3,2,1,0:T(8,128)} fusion(f32[5,8,128,256]{3,2,1,0:T(8,128)} %param.7, f32[5,8,128,1]{3,2,1,0:T(8,128)S(1)} %copy-done.6, f32[5,8,128,1]{3,2,1,0:T(8,128)} %slice_multiply_fusion.2, f32[5,10,128,256]{3,2,1,0:T(8,128)S(1)} %bitcast.67, f32[5,10,1,256]{3,2,1,0:T(1,128)S(1)} %collective-permute-done.2, ...), kind=kLoop, calls=%fused_computation.42 | loop fusion | flops 48496640 | bytes 52053032 | tf_op jit(solution)/shard_map/add | solution.py:186
  (144 shorter events, 24.7 us)
Async XLA Ops:
  7.2 100.4 %reduce-scatter.2.cloned.1.call-start = ((), (), s32[]{:S(2)}) async-start(), calls=%async_computation.1 | async-start | bytes 348160 | tf_op jit(solution)/shard_map/reduce_scatter | solution.py:169
  11.0 26.7 %copy-start.9 = (f32[5,8,12,192]{3,1,2,0:T(8,128)S(1)}, f32[5,8,12,192]{3,1,2,0:T(8,128)}, u32[]{:S(2)}) copy-start(f32[5,8,12,192]{3,1,2,0:T(8,128)} %param.8) | copy-start | bytes 1105924
  32.3 12.8 %copy-start.26 = (f32[5]{0:T(128)S(1)}, f32[5]{0:T(128)}, u32[]{:S(2)}) copy-start(f32[5]{0:T(128)} %constant.21.clone) | copy-start | bytes 64
  34.8 27.9 %collective-permute-start = (f32[5,1,128,256]{3,2,1,0:T(8,128)}, f32[5,1,128,256]{3,2,1,0:T(8,128)S(1)}, u32[]{:S(2)}, u32[]{:S(2)}) collective-permute-start(f32[5,1,128,256]{3,2,1,0:T(8,128)} %get-tuple-element.50), channel_id=1, source_target_pairs={{0,16},{16,32},{32,48},{48,64},{64,80},{80,96},{96,112},{112,0},{1... | collective-permute-start | bytes 1966088 | tf_op jit(solution)/shard_map/ppermute | solution.py:23
  34.8 32.0 %collective-permute-start.1 = (f32[5,1,128,256]{3,2,1,0:T(8,128)}, f32[5,1,128,256]{3,2,1,0:T(8,128)S(1)}, u32[]{:S(2)}, u32[]{:S(2)}) collective-permute-start(f32[5,1,128,256]{3,2,1,0:T(8,128)} %get-tuple-element.49), channel_id=1, source_target_pairs={{16,0},{32,16},{48,32},{64,48},{80,64},{96,80},{112,96},{0,112},{1... | collective-permute-start | bytes 1966088 | tf_op jit(solution)/shard_map/ppermute | solution.py:26
  37.8 17.1 %collective-permute-start.5 = (f32[5,1,12,192]{3,1,0,2:T(1,128)S(1)}, f32[5,1,12,192]{3,1,0,2:T(1,128)S(1)}, u32[]{:S(2)}, u32[]{:S(2)}) collective-permute-start(f32[5,1,12,192]{3,1,0,2:T(1,128)S(1)} %get-tuple-element.54), channel_id=1, source_target_pairs={{16,0},{32,16},{48,32},{64,48},{80,64},{96,80},{112,96},{0,112},{1... | collective-permute-start | bytes 138248 | tf_op jit(solution)/shard_map/ppermute | solution.py:26
  37.8 17.0 %collective-permute-start.4 = (f32[5,1,12,192]{3,1,0,2:T(1,128)S(1)}, f32[5,1,12,192]{3,1,0,2:T(1,128)S(1)}, u32[]{:S(2)}, u32[]{:S(2)}) collective-permute-start(f32[5,1,12,192]{3,1,0,2:T(1,128)S(1)} %get-tuple-element.53), channel_id=1, source_target_pairs={{0,16},{16,32},{32,48},{48,64},{64,80},{80,96},{96,112},{112,0},{1... | collective-permute-start | bytes 138248 | tf_op jit(solution)/shard_map/ppermute | solution.py:23
  45.1 8.5 %copy-start.24 = (f32[768,4]{0,1:T(4,128)S(1)}, f32[768,4]{0,1:T(4,128)}, u32[]{:S(2)}) copy-start(f32[768,4]{0,1:T(4,128)} %param.10) | copy-start | bytes 36868
  45.1 8.6 %copy-start.25 = (s32[768,4]{0,1:T(4,128)S(1)}, s32[768,4]{0,1:T(4,128)}, u32[]{:S(2)}) copy-start(s32[768,4]{0,1:T(4,128)} %param.9) | copy-start | bytes 36868
  54.9 7.5 %copy-start.19 = (f32[5,1,12,192]{3,1,0,2:T(1,128)}, f32[5,1,12,192]{3,1,0,2:T(1,128)S(1)}, u32[]{:S(2)}) copy-start(f32[5,1,12,192]{3,1,0,2:T(1,128)S(1)} %collective-permute-done.5) | copy-start | bytes 138244
  54.9 7.5 %copy-start.21 = (f32[5,1,12,192]{3,1,0,2:T(1,128)}, f32[5,1,12,192]{3,1,0,2:T(1,128)S(1)}, u32[]{:S(2)}) copy-start(f32[5,1,12,192]{3,1,0,2:T(1,128)S(1)} %collective-permute-done.4) | copy-start | bytes 138244
  55.6 109.2 %collective-permute-start.7 = (f32[5,10,1,192]{3,1,0,2:T(8,128)}, f32[5,10,1,192]{3,1,0,2:T(8,128)}, u32[]{:S(2)}, u32[]{:S(2)}) collective-permute-start(f32[5,10,1,192]{3,1,0,2:T(8,128)} %get-tuple-element.51), channel_id=1, source_target_pairs={{1,0},{2,1},{3,2},{4,3},{5,4},{6,5},{7,6},{8,7},{9,8},{10,9},{11,1... | collective-permute-start | bytes 115208 | tf_op jit(solution)/shard_map/ppermute | solution.py:26
  62.2 102.6 %collective-permute-start.6 = (f32[5,10,1,192]{3,1,0,2:T(8,128)}, f32[5,10,1,192]{3,1,0,2:T(8,128)}, u32[]{:S(2)}, u32[]{:S(2)}) collective-permute-start(f32[5,10,1,192]{3,1,0,2:T(8,128)} %get-tuple-element.52), channel_id=1, source_target_pairs={{0,1},{1,2},{2,3},{3,4},{4,5},{5,6},{6,7},{7,8},{8,9},{9,10},{10,1... | collective-permute-start | bytes 115208 | tf_op jit(solution)/shard_map/ppermute | solution.py:23
  66.8 42.2 %copy-start.15 = (f32[5,1,128,256]{3,2,1,0:T(8,128)}, f32[5,1,128,256]{3,2,1,0:T(8,128)S(1)}, u32[]{:S(2)}) copy-start(f32[5,1,128,256]{3,2,1,0:T(8,128)S(1)} %collective-permute-done.1) | copy-start | bytes 1966084
  109.7 11.1 %copy-start.5 = (f32[5,8,128,1]{3,2,1,0:T(8,128)}, f32[5,8,128,1]{3,2,1,0:T(8,128)S(1)}, u32[]{:S(2)}) copy-start(f32[5,8,128,1]{3,2,1,0:T(8,128)S(1)} %copy.31) | copy-start | bytes 61444
  109.8 62.8 %collective-permute-start.2 = (f32[5,10,1,256]{3,2,1,0:T(1,128)}, f32[5,10,1,256]{3,2,1,0:T(1,128)S(1)}, u32[]{:S(2)}, u32[]{:S(2)}) collective-permute-start(f32[5,10,1,256]{3,2,1,0:T(1,128)} %get-tuple-element.41), channel_id=1, source_target_pairs={{0,1},{1,2},{2,3},{3,4},{4,5},{5,6},{6,7},{7,8},{8,9},{9,10},{10,1... | collective-permute-start | bytes 153608 | tf_op jit(solution)/shard_map/ppermute | solution.py:23
  111.0 61.6 %collective-permute-start.3 = (f32[5,10,1,256]{3,2,1,0:T(1,128)}, f32[5,10,1,256]{3,2,1,0:T(1,128)S(1)}, u32[]{:S(2)}, u32[]{:S(2)}) collective-permute-start(f32[5,10,1,256]{3,2,1,0:T(1,128)} %get-tuple-element.40), channel_id=1, source_target_pairs={{1,0},{2,1},{3,2},{4,3},{5,4},{6,5},{7,6},{8,7},{9,8},{10,9},{11,1... | collective-permute-start | bytes 153608 | tf_op jit(solution)/shard_map/ppermute | solution.py:26
  121.3 5.1 %copy-start.2 = (f32[1,8,128,258]{3,2,1,0:T(8,128)}, f32[1,8,128,258]{3,2,1,0:T(8,128)S(1)}, u32[]{:S(2)}) copy-start(f32[1,8,128,258]{3,2,1,0:T(8,128)S(1)} %get-tuple-element.39) | copy-start | bytes 3170308
  121.4 5.3 %slice-start = ((s8[6553600]{0:T(1024)(128)(4,1)}), s8[4194304]{0:T(1024)(128)(4,1)S(1)}, s32[]{:S(2)}) async-start(s8[6553600]{0:T(1024)(128)(4,1)} %bitcast.64), calls=%async_computation.2 | async-start | bytes 8388608
  131.7 31.7 %copy-start.7 = (f32[1,10,128,256]{3,2,1,0:T(8,128)}, f32[1,10,128,256]{3,2,1,0:T(8,128)S(1)}, u32[]{:S(2)}) copy-start(f32[1,10,128,256]{3,2,1,0:T(8,128)S(1)} %get-tuple-element.26) | copy-start | bytes 3932164
  163.5 6.0 %slice-start.2 = ((s8[6553600]{0:T(1024)(128)(4,1)}), s8[2359296]{0:T(1024)(128)(4,1)S(1)}, s32[]{:S(2)}) async-start(s8[6553600]{0:T(1024)(128)(4,1)} %bitcast.66), calls=%async_computation.4 | async-start | bytes 4718592
  164.7 4.7 %copy-start.8 = (f32[1,10,128,256]{3,2,1,0:T(8,128)S(1)}, f32[1,10,128,256]{3,2,1,0:T(8,128)}, u32[]{:S(2)}) copy-start(f32[1,10,128,256]{3,2,1,0:T(8,128)} %copy-done.7) | copy-start | bytes 3932164
  164.7 4.7 %copy-start.12 = (f32[1,10,128,256]{3,2,1,0:T(8,128)S(1)}, f32[1,10,128,256]{3,2,1,0:T(8,128)}, u32[]{:S(2)}) copy-start(f32[1,10,128,256]{3,2,1,0:T(8,128)} %get-tuple-element.27) | copy-start | bytes 3932164
  166.4 4.6 %copy-start.22 = (f32[5,1,12,192]{3,1,0,2:T(1,128)S(1)}, f32[5,1,12,192]{3,1,0,2:T(1,128)}, u32[]{:S(2)}) copy-start(f32[5,1,12,192]{3,1,0,2:T(1,128)} %copy-done.21) | copy-start | bytes 138244
  (16 other events, 51.8 us)
Sparse Core Ops, SparseCore 0:
  32.4 75.0 reduce-scatter.1
where the time goes:
time: 210 us; the launch traced here: 209 us
  other arithmetic  60.7 us (29%)
  waiting for transfers between devices  36.8 us (18%)
  local copies, waits for them, and re-layouts  31.5 us (15%)
  matrix products  27.9 us (13%)
  blocking collectives  22.2 us (11%)
  starting transfers between devices  15.5 us (7%)
  between operations  14.7 us (7%)
    reduce_scatter x1, waiting for transfers between devices, body(): lax.psum_scatter(cycle_share, 'azim', scatter_dimension=2, tiled=True)  36.8 us
    dot_general x2, matrix products, apply_taps(): jnp.dot(flat_values, matrix, preferred_element_type=jnp.float32, precisio...  27.9 us
    add x1, other arithmetic, body(): cycle_state + time_step * cycle_rhs(padded, inner_ghost, angle_step)  25.6 us
    unnamed x79, local copies, waits for them, and re-layouts  22.5 us
    all_gather x1, blocking collectives, body(): all_traces = lax.all_gather(cart_trace, 'azim', axis=2, tiled=True)  22.2 us
    ppermute x4, starting transfers between devices, padded_2(): lax.ppermute(lax.slice_in_dim(block, 0, width, axis=dim), axis, backward)  13.8 us
    unnamed x22, other arithmetic  9.48 us
    concatenate x1, other arithmetic, cycle_rhs(): jnp.concatenate([inner_ghost[..., None], center, outer_ghost[..., None]],...  5.68 us
  transfers between devices with their start and end apart: 9, of which 1 were waited for; matrix products, arithmetic and copies ran while one was open for 27% of the time, Pallas kernels for 0%

commit v1 on v0

v1 whole, which is shorter than its diff:
```python
import functools
import math

import jax
import jax.numpy as jnp
import numpy as np
from jax import lax
from jax.experimental import pallas as pl
from jax.experimental.pallas import tpu as pltpu
from jax.sharding import PartitionSpec as P

DT = 0.001
DX = 0.004
DR = 1.0 / 256.0
DC = 2.0 / 192.0
NU = 0.002
NT = 2048
NR = 256
NC = 192
PL = 8
SEC = 128
ROWS = 12
NA = 16
DA = 2.0 * math.pi / NT

BX = NU * DT / DX**2
AX = DT / (2.0 * DX)
BR = NU * DT / DR**2 / BX
AC = DT / (2.0 * DC) / BX
BC = NU * DT / DC**2 / BX
SX = DX / (2.0 * NU)


def tables():
    radius = lambda i: 1.0 + (i + 0.5) / 256.0
    i = np.arange(NR, dtype=np.float64)
    tab = np.zeros((8, NR))
    tab[0] = DT / (2.0 * DA * radius(i)) / BX
    tab[1] = NU * DT / (DA * radius(i)) ** 2 / BX
    tab[2] = DT * radius(i) / (2.0 * DR * radius(i - 1)) / BX
    tab[3] = DT * radius(i) / (2.0 * DR * radius(i + 1)) / BX
    tab[3, -1] = DT * radius(NR) / (2.0 * DR * radius(NR - 1)) / BX
    tab[4] = 1.0 / BX - 2.0 - 2.0 * BR - 2.0 * tab[1]
    tab[5] = DT / radius(i) / BX
    angle = (np.arange(NT) + 0.5) * (2.0 * math.pi / NT)
    trig = np.zeros((8, NT))
    trig[0] = np.cos(angle)
    trig[1] = np.sin(angle)
    return tab.astype(np.float32), trig.astype(np.float32)


INNER = float(DT * (1.0 - 0.5 / 256.0) / (2.0 * DR * (1.0 + 0.5 / 256.0)) / BX)
CC = float(1.0 / BX - 2.0 - 4.0 * BC)


def needed(a):
    found = set()
    for off in (0, 512):
        found |= {((32 * a - 8 + off) // SEC) % NA, ((32 * a + 37 + off) // SEC) % NA}
    if a == 0:
        found |= set(range(7, 13))
    if a == NA - 1:
        found |= {11, 12, 13, 14, 15, 0}
    return sorted(found)


def point(q):
    inv = pl.reciprocal(q[0], approx=False)
    u1, u2, u3 = q[1] * inv, q[2] * inv, q[3] * inv
    p11, p22, p33 = q[1] * u1, q[2] * u2, q[3] * u3
    pr = 0.4 * q[4] - 0.2 * (p11 + p22 + p33)
    return (u1, u2, u3), (p11, p22, p33), pr, q[4] + pr


def flux(q, pt, k):
    u, sq, pr, h = pt
    v = u[k - 1]
    out = [q[k], q[1] * v, q[2] * v, q[3] * v, h * v]
    out[k] = sq[k - 1] + pr
    return out


def kernel(
    cyc, cor, ctaps, cwts, ytaps, ywts, tab_in, trig_in, cyc_out, cor_out,
    qv, ov, p2s, m2s, ah, cin, cv, oc, chx, crlo, crhi, cres, trs, trr, shs, shr, xm,
    gl, gr, tab, trig, ct, cw, yt, yw,
    in_sem, sm_sem, out_sem, ax_s, ax_r, cx_s, cx_r, ar_s, ar_r, cr_s, cr_r, tr_s, tr_r, sh_s, sh_r,
):
    me = lax.axis_index("azim")
    ax = lax.axis_index("axial")
    n_ax = lax.axis_size("axial")
    up_ax = {"axial": lax.rem(ax + 1, n_ax)}
    dn_ax = {"axial": lax.rem(ax + n_ax - 1, n_ax)}
    up_az = {"azim": lax.rem(me + 1, NA)}
    dn_az = {"azim": lax.rem(me + NA - 1, NA)}
    MESH = pl.DeviceIdType.MESH

    barrier = pltpu.get_barrier_semaphore()
    pl.semaphore_signal(barrier, inc=1, device_id=up_ax, device_id_type=MESH)
    pl.semaphore_signal(barrier, inc=1, device_id=dn_ax, device_id_type=MESH)

    def greet(d, _):
        @pl.when(d != me)
        def _():
            pl.semaphore_signal(barrier, inc=1, device_id={"azim": d}, device_id_type=MESH)

        return 0

    lax.fori_loop(0, NA, greet, 0)

    smalls = [
        pltpu.make_async_copy(s, d, sm_sem.at[i])
        for i, (s, d) in enumerate(
            [(cor, cin), (ytaps, yt), (ywts, yw), (tab_in, tab), (trig_in, trig), (ctaps, ct), (cwts, cw)]
        )
    ]
    planes = [pltpu.make_async_copy(cyc.at[:, p], qv.at[:, p + 1], in_sem.at[p]) for p in range(PL)]
    for c in smalls:
        c.start()
    for c in planes:
        c.start()

    def remote(src, dst, s, r, dev):
        return pltpu.make_async_remote_copy(
            src_ref=src, dst_ref=dst, send_sem=s, recv_sem=r, device_id=dev, device_id_type=MESH
        )

    axial = [
        remote(cyc.at[:, 0], qv.at[:, PL + 1], ax_s.at[0], ax_r.at[0], dn_ax),
        remote(cyc.at[:, PL - 1], qv.at[:, 0], ax_s.at[1], ax_r.at[1], up_ax),
    ]
    caxial = [
        remote(cor.at[:, :, 0, :], chx.at[:, :, PL - 1, :], cx_s.at[0], cx_r.at[0], dn_ax),
        remote(cor.at[:, :, PL - 1, :], chx.at[:, :, 0, :], cx_s.at[1], cx_r.at[1], up_ax),
    ]
    azim = [
        remote(cyc.at[:, :, 0, :], ah.at[:, :, 7, :], ar_s.at[0], ar_r.at[0], dn_az),
        remote(cyc.at[:, :, SEC - 1, :], ah.at[:, :, 0, :], ar_s.at[1], ar_r.at[1], up_az),
    ]
    crow_dn = remote(cor.at[:, 0], crhi, cr_s.at[0], cr_r.at[0], dn_az)
    crow_up = remote(cor.at[:, ROWS - 1], crlo, cr_s.at[1], cr_r.at[1], up_az)

    lane8 = lax.broadcasted_iota(jnp.int32, (8, 128), 1)
    row8 = lax.broadcasted_iota(jnp.int32, (8, 128), 0)

    pl.semaphore_wait(barrier, NA - 1 + 2)
    for c in axial:
        c.start()
    for c in azim + caxial:
        c.start()

    @pl.when(me > 0)
    def _():
        crow_dn.start()

    @pl.when(me < NA - 1)
    def _():
        crow_up.start()

    for c in smalls:
        c.wait()

    def pad(i, _):
        for c in range(5):
            cv[c, i + 1, :, 0:128] = cin[c, i, :, 0:128]
            cv[c, i + 1, :, 128:192] = cin[c, i, :, 128:192]
        return 0

    lax.fori_loop(0, ROWS, pad, 0)

    for c in planes:
        c.wait()

    lane_s = lax.broadcasted_iota(jnp.int32, (SEC, 128), 1)

    def trace(p, t):
        for c in range(5):
            ch = c * 8 + p
            t = jnp.where(lane_s == ch, pltpu.roll(qv[c, p + 1, :, 0:128], ch, 1), t)
        return t

    tt = lax.fori_loop(0, PL, trace, jnp.zeros((SEC, 128), jnp.float32)).T
    own = pl.ds(pl.multiple_of(me * SEC, SEC), SEC)
    cosine = jnp.broadcast_to(trig[0:1, own], (8, 128))
    sine = jnp.broadcast_to(trig[1:2, own], (8, 128))
    tq = [tt[8 * c : 8 * c + 8, :] for c in range(5)]
    cart = [tq[0], tq[1], tq[3] * cosine - tq[2] * sine, tq[3] * sine + tq[2] * cosine, tq[4]]
    for c in range(5):
        trs[c] = cart[c]
        trr[me, c] = cart[c]

    def tr_copy(d):
        return remote(trs, trr.at[me], tr_s.at[d], tr_r.at[me], {"azim": d})

    def is_in(x, items):
        hit = x == items[0]
        for it in items[1:]:
            hit = jnp.logical_or(hit, x == it)
        return hit

    for a in range(NA):
        others = [s for s in needed(a) if s != a]

        @pl.when(is_in(me, others))
        def _(a=a):
            tr_copy(a).start()

    vcol = []
    for c in range(5):
        v = jnp.zeros((8, 128), jnp.float32)
        for i in range(ROWS):
            left = pltpu.roll(cv[c, i + 1, :, 0:128], 8 * i, 1)
            right = pltpu.roll(cv[c, i + 1, :, 128:256], (8 * i + 4 - 60) % 128, 1)
            v = jnp.where((lane8 >> 3) == i, jnp.where((lane8 & 7) < 4, left, right), v)
        vcol.append(v)
    for c in range(5):
        xm[c * 8 : c * 8 + 8, :] = vcol[c]

    def bcast(x):
        return jnp.broadcast_to(x, (8, 128))

    edge = jnp.logical_or(me == 0, me == NA - 1)
    r0 = jnp.where(me == 0, 0, ROWS - 4)

    def share(d, _):
        cols = pl.ds(pl.multiple_of(d * SEC, SEC), SEC)
        ws = [yw[k : k + 1, cols] for k in range(4)]
        total = ws[0] + ws[1] + ws[2] + ws[3]
        acc = [jnp.zeros((8, 128), jnp.float32) for _ in range(5)]
        for k in range(4):
            tap = bcast(yt[k : k + 1, cols])
            w = bcast(ws[k] / total)
            row = ((tap >> 6) * 43691) >> 17
            col = tap - row * NC
            lrow = row - me * ROWS
            inside = jnp.logical_and(lrow >= 0, lrow < ROWS)
            side = jnp.logical_or(col < 4, col >= NC - 4)
            ok = jnp.logical_and(inside, side)
            idx = (lrow * 8 + jnp.where(col < 4, col, col - (NC - 8))) & 127
            wk = jnp.where(ok, w, 0.0)
            for c in range(5):
                got = jnp.take_along_axis(xm[c * 8 : c * 8 + 8, :], idx, axis=1)
                acc[c] = acc[c] + wk * got
        for c in range(5):
            shs[d, c] = acc[c]

        @pl.when(edge)
        def _():
            extra = [jnp.zeros((8, 128), jnp.float32) for _ in range(5)]
            for k in range(4):
                tap = bcast(yt[k : k + 1, cols])
                w = bcast(ws[k] / total)
                row = ((tap >> 6) * 43691) >> 17
                col = tap - row * NC
                erow = row - me * ROWS - r0
                mid = jnp.logical_and(col >= 4, col < NC - 4)
                idx = col & 127
                high = col >= 128
                for r in range(4):
                    wk = jnp.where(jnp.logical_and(mid, erow == r), w, 0.0)
                    for c in range(5):
                        lo = jnp.take_along_axis(cv[c, r0 + r + 1, :, 0:128], idx, axis=1)
                        hi = jnp.take_along_axis(cv[c, r0 + r + 1, :, 128:256], idx, axis=1)
                        extra[c] = extra[c] + wk * jnp.where(high, hi, lo)
            for c in range(5):
                shs[d, c] += extra[c]

        @pl.when(d != me)
        def _():
            sh_copy(d).start()

        @pl.when(d == me)
        def _():
            for c in range(5):
                shr[d, c] = shs[d, c]

        return 0

    def sh_copy(d):
        return remote(shs.at[d], shr.at[me], sh_s.at[d], sh_r.at[me], {"azim": d})

    lax.fori_loop(0, NA, share, 0)

    lane = lax.broadcasted_iota(jnp.int32, (8, 128), 1)
    first, last = lane == 0, lane == 127

    zero8 = jnp.zeros((8, 128), jnp.float32)
    for c in range(5):
        for h in range(2):
            m2s[c, h, 8:16, :] = zero8
            p2s[c, h, 144:152, :] = zero8

    def clear(b, _):
        rows = pl.ds(pl.multiple_of(b * 8, 8), 8)
        for c in range(5):
            ov[c, 1, rows, :] = jnp.zeros((8, NR), jnp.float32)
        return 0

    lax.fori_loop(1, 17, clear, 0)

    def finish(p, b):
        rows = pl.ds(pl.multiple_of((b + 1) * 8, 8), 8)
        for c in range(5):
            for h in range(2):
                half = slice(128 * h, 128 * h + 128)
                up = p2s[c, h, pl.ds(b * 8 + 17, 8), :]
                dn = m2s[c, h, pl.ds(b * 8 + 15, 8), :]
                ov[c, p + 1, rows, half] += up + dn

    def cycle_plane(p, _):
        def block(b, _):
            src = pl.ds(pl.multiple_of(b * 8, 8), 8)
            rows = pl.ds(pl.multiple_of((b + 1) * 8, 8), 8)
            srows = pl.ds(pl.multiple_of((b + 2) * 8, 8), 8)
            q = [qv[c, p + 1, src, :] for c in range(5)]
            pt = point(q)
            f1, f2, f3 = flux(q, pt, 1), flux(q, pt, 2), flux(q, pt, 3)
            row = lambda k: jnp.broadcast_to(tab[k : k + 1, :], (8, NR))
            ka, ba, cp, cm, cc, so = [row(k) for k in range(6)]
            for c in range(5):
                m1 = q[c] + f1[c]
                p1 = q[c] - f1[c]
                ov[c, p, rows, :] = BX * (ov[c, p, rows, :] + p1)
                acc = ov[c, p + 1, rows, :] + cc * q[c]
                ov[c, p + 2, rows, :] = m1
                base = BR * q[c]
                p3 = base - cp * f3[c]
                m3 = base + cm * f3[c]
                a, bb = pltpu.roll(p3[:, :128], 127, 1), pltpu.roll(p3[:, 128:], 127, 1)
                wall = m3[:, 128:] if c != 3 else -m3[:, 128:]
                e, f = pltpu.roll(m3[:, :128], 1, 1), pltpu.roll(m3[:, 128:], 1, 1)
                lo = jnp.where(last, bb, a) + jnp.where(first, 0.0, e)
                hi = jnp.where(last, wall, bb) + jnp.where(first, e, f)
                acc = acc + jnp.concatenate([lo, hi], axis=1)
                if c == 2:
                    acc = acc - so * f2[3]
                if c == 3:
                    acc = acc + so * f2[2]
                ov[c, p + 1, rows, :] = acc
                bq = ba * q[c]
                kf = ka * f2[c]
                p2, m2 = bq - kf, bq + kf
                for h in range(2):
                    half = slice(128 * h, 128 * h + 128)
                    p2s[c, h, srows, :] = p2[:, half]
                    m2s[c, h, srows, :] = m2[:, half]
            finish(p, b - 1)
            return 0

        lax.fori_loop(0, SEC // 8, block, 0)
        for c in range(5):
            for h in range(2):
                p2s[c, h, 144:152, :] = zero8
        finish(p, SEC // 8 - 1)
        return 0

    lax.fori_loop(0, PL, cycle_plane, 0)

    for s in range(NA):
        takers = [a for a in range(NA) if s in needed(a) and a != s]

        @pl.when(is_in(me, takers))
        def _(s=s):
            remote(trs, trr.at[s], tr_s.at[s], tr_r.at[s], {"azim": s}).wait_recv()

    s0 = ((32 * me + 2040) >> 7) & 15
    s1 = ((32 * me + 37) >> 7) & 15

    def ghost(start, shift, sectors):
        vals = [zero8 for _ in range(5)]
        ws = [bcast_roll(cw[k : k + 1, start : start + 256], shift) for k in range(4)]
        total = ws[0] + ws[1] + ws[2] + ws[3]
        for k in range(4):
            tap = bcast_roll(ct[k : k + 1, start : start + 256], shift)
            idx = tap & 127
            sec = tap >> 7
            w = ws[k] / total
            for c in range(5):
                v = jnp.take_along_axis(trr[sectors[0], c], idx, axis=1)
                for s in sectors[1:]:
                    v = jnp.where(sec == s, jnp.take_along_axis(trr[s, c], idx, axis=1), v)
                vals[c] = vals[c] + w * v
        return vals

    def bcast_roll(x, shift):
        full = jnp.broadcast_to(x, (8, 256))
        if isinstance(shift, int):
            return full[:, shift : shift + 128]
        return pltpu.roll(full, shift, 1)[:, :128]

    def col_terms(g):
        pt = point(g)
        return flux(g, pt, 3)

    back = lax.rem(512 - ROWS * me, 256)
    g = ghost(0, back, [s0, s1])
    f = col_terms(g)
    for c in range(5):
        gl[c] = BC * g[c] + AC * f[c]
    back = lax.rem(512 - 64 - ROWS * me, 256)
    g = ghost(128, back, [(s0 + 4) & 15, (s1 + 4) & 15])
    f = col_terms(g)
    for c in range(5):
        gr[c] = BC * g[c] - AC * f[c]

    @pl.when(me > 0)
    def _():
        crow_up.wait_recv()
        for c in range(5):
            cv[c, 0, :, 0:128] = crlo[c, :, 0:128]
            cv[c, 0, :, 128:192] = crlo[c, :, 128:192]

    @pl.when(me < NA - 1)
    def _():
        crow_dn.wait_recv()
        for c in range(5):
            cv[c, ROWS + 1, :, 0:128] = crhi[c, :, 0:128]
            cv[c, ROWS + 1, :, 128:192] = crhi[c, :, 128:192]

    @pl.when(me == 0)
    def _():
        for h in range(2):
            g = ghost(384, 0, list(range(7, 13))) if h == 0 else ghost(384, 128, list(range(7, 13)))
            for c in range(5):
                cv[c, 0, :, 128 * h : 128 * h + 128] = g[c]

    @pl.when(me == NA - 1)
    def _():
        g = ghost(512, 64, [11, 12, 13, 14, 15, 0])
        for c in range(5):
            cv[c, ROWS + 1, :, 0:128] = g[c]
        g = ghost(512, 128, [11, 12, 13, 14, 15, 0])
        for c in range(5):
            cv[c, ROWS + 1, :, 128:256] = pltpu.roll(g[c], 64, 1)

    for c in caxial:
        c.wait_recv()

    for c in range(5):
        oc[c, 1] = jnp.zeros((8, 256), jnp.float32)

    def core_row(i, _):
        q = [cv[c, i, :, :] for c in range(5)]
        pt = point(q)
        f1, f2, f3 = flux(q, pt, 1), flux(q, pt, 2), flux(q, pt, 3)
        for h in range(2):
            half = slice(128 * h, 128 * h + (128 if h == 0 else 64))
        x = [chx[c, i - 1, :, :] for c in range(5)]
        x = [jnp.concatenate([v, jnp.ones((8, 64), jnp.float32)], axis=1) for v in x]
        xf = flux(x, point(x), 1)
        sub = lax.broadcasted_iota(jnp.int32, (8, 256), 0)
        for c in range(5):
            m1 = pltpu.roll(q[c] + f1[c], 1, 0)
            p1 = pltpu.roll(q[c] - f1[c], 7, 0)
            m1 = jnp.where(sub == 0, x[c] + xf[c], m1)
            p1 = jnp.where(sub == 7, x[c] - xf[c], p1)
            acc = oc[c, i] + CC * q[c] + m1 + p1
            base = BC * q[c]
            p3, m3 = base - AC * f3[c], base + AC * f3[c]
            a, bb = pltpu.roll(p3[:, :128], 127, 1), pltpu.roll(p3[:, 128:], 127, 1)
            e, f = pltpu.roll(m3[:, :128], 1, 1), pltpu.roll(m3[:, 128:], 1, 1)
            lg = pltpu.roll(gl[c], lax.rem(129 - i, 128), 1)
            rg = pltpu.roll(gr[c], lax.rem(64 + 128 - i, 128), 1)
            lo = jnp.where(last, bb, a) + jnp.where(first, lg, e)
            hi = jnp.where(lane == 63, rg, bb) + jnp.where(first, e, f)
            acc = acc + jnp.concatenate([lo, hi], axis=1)
            p2, m2 = base - AC * f2[c], base + AC * f2[c]
            oc[c, i - 1] = BX * (oc[c, i - 1] + p2)
            oc[c, i] = acc
            oc[c, i + 1] = m2
        return 0

    q = [cv[c, 0, :, :] for c in range(5)]
    f2 = flux(q, point(q), 2)
    for c in range(5):
        oc[c, 1] = BC * q[c] + AC * f2[c]
    lax.fori_loop(1, ROWS + 1, core_row, 0)
    q = [cv[c, ROWS + 1, :, :] for c in range(5)]
    f2 = flux(q, point(q), 2)
    for c in range(5):
        oc[c, ROWS] = BX * (oc[c, ROWS] + BC * q[c] - AC * f2[c])

    def unpad(i, _):
        for c in range(5):
            cres[c, i, :, 0:128] = oc[c, i + 1, :, 0:128]
            cres[c, i, :, 128:192] = oc[c, i + 1, :, 128:192]
        return 0

    lax.fori_loop(0, ROWS, unpad, 0)
    core_done = pltpu.make_async_copy(cres, cor_out, out_sem.at[PL])
    core_done.start()

    def await_share(d, _):
        @pl.when(d != me)
        def _():
            remote(shs.at[d], shr.at[d], sh_s.at[d], sh_r.at[d], {"azim": d}).wait_recv()

        return 0

    lax.fori_loop(0, NA, await_share, 0)
    cart = [functools.reduce(jnp.add, [shr[d, c] for d in range(NA)]) for c in range(5)]
    g = [cart[0], cart[1], cart[3] * cosine - cart[2] * sine, cart[2] * cosine + cart[3] * sine, cart[4]]
    f3 = flux(g, point(g), 3)
    for c in range(5):
        xm[8 * c : 8 * c + 8, :] = BR * g[c] + INNER * f3[c]
    fix = xm[...].T
    for c in azim:
        c.wait_recv()

    def patch(p, _):
        scale = jnp.where(p == PL - 1, 1.0, BX).astype(jnp.float32)
        for c in range(5):
            col = pltpu.roll(fix, lax.rem(128 - (8 * c + p), 128), 1)
            ov[c, p + 1, 8 : 8 + SEC, 0:128] += jnp.where(lane_s == 0, col * scale, 0.0)
        q = [ah[c, p, :, :] for c in range(5)]
        f2 = flux(q, point(q), 2)
        sub = lax.broadcasted_iota(jnp.int32, (8, NR), 0)
        ka = jnp.broadcast_to(tab[0:1, :], (8, NR))
        ba = jnp.broadcast_to(tab[1:2, :], (8, NR))
        for c in range(5):
            bq, kf = ba * q[c], ka * f2[c]
            ov[c, p + 1, 8:16, :] += jnp.where(sub == 0, (bq + kf) * scale, 0.0)
            ov[c, p + 1, SEC : SEC + 8, :] += jnp.where(sub == 7, (bq - kf) * scale, 0.0)
        return 0

    lax.fori_loop(0, PL, patch, 0)
    outs = [
        pltpu.make_async_copy(ov.at[:, p + 1, 8 : 8 + SEC, :], cyc_out.at[:, p], out_sem.at[p])
        for p in range(PL)
    ]
    for p in range(1, PL - 1):
        outs[p].start()

    for c in axial:
        c.wait_recv()

    def ends(b, _):
        src = pl.ds(pl.multiple_of(b * 8, 8), 8)
        rows = pl.ds(pl.multiple_of((b + 1) * 8, 8), 8)
        q = [qv[c, 0, src, :] for c in range(5)]
        f1 = flux(q, point(q), 1)
        for c in range(5):
            ov[c, 1, rows, :] += BX * (q[c] + f1[c])
        q = [qv[c, PL + 1, src, :] for c in range(5)]
        f1 = flux(q, point(q), 1)
        for c in range(5):
            ov[c, PL, rows, :] = BX * (ov[c, PL, rows, :] + (q[c] - f1[c]))
        return 0

    lax.fori_loop(0, SEC // 8, ends, 0)
    outs[0].start()
    outs[PL - 1].start()

    for c in axial + azim + caxial:
        c.wait_send()

    @pl.when(me > 0)
    def _():
        crow_dn.wait_send()

    @pl.when(me < NA - 1)
    def _():
        crow_up.wait_send()

    for a in range(NA):
        others = [s for s in needed(a) if s != a]

        @pl.when(is_in(me, others))
        def _(a=a):
            tr_copy(a).wait_send()

    def drain(d, _):
        @pl.when(d != me)
        def _():
            sh_copy(d).wait_send()

        return 0

    lax.fori_loop(0, NA, drain, 0)
    core_done.wait()
    for c in outs:
        c.wait()


def body(cycle_state, core_state, core_taps, core_weights, cycle_taps, cycle_weights):
    tab, trig = tables()
    f32, i32 = jnp.float32, jnp.int32
    dma = pltpu.SemaphoreType.DMA
    core_t = jnp.transpose(core_state, (0, 2, 1, 3))
    hbm = pl.BlockSpec(memory_space=pl.ANY)
    vm = pltpu.VMEM
    cycle_new, core_new = pl.pallas_call(
        kernel,
        out_shape=(
            jax.ShapeDtypeStruct(cycle_state.shape, f32),
            jax.ShapeDtypeStruct(core_t.shape, f32),
        ),
        in_specs=[hbm] * 8,
        out_specs=(hbm, hbm),
        scratch_shapes=[
            vm((5, PL + 2, SEC, NR), f32),
            vm((5, PL + 2, SEC + 8, NR), f32),
            vm((5, 2, SEC + 24, 128), f32),
            vm((5, 2, SEC + 24, 128), f32),
            vm((5, PL, 8, NR), f32),
            vm((5, ROWS, PL, NC), f32),
            vm((5, ROWS + 2, PL, 256), f32),
            vm((5, ROWS + 2, PL, 256), f32),
            vm((5, ROWS, PL, NC), f32),
            vm((5, PL, NC), f32),
            vm((5, PL, NC), f32),
            vm((5, ROWS, PL, NC), f32),
            vm((5, 8, 128), f32),
            vm((NA, 5, 8, 128), f32),
            vm((NA, 5, 8, 128), f32),
            vm((NA, 5, 8, 128), f32),
            vm((128, 128), f32),
            vm((5, 8, 128), f32),
            vm((5, 8, 128), f32),
            vm((8, NR), f32),
            vm((8, NT), f32),
            vm((4, 768), i32),
            vm((4, 768), f32),
            vm((4, NT), i32),
            vm((4, NT), f32),
            dma((PL,)),
            dma((7,)),
            dma((PL + 1,)),
            dma((2,)), dma((2,)), dma((2,)), dma((2,)), dma((2,)), dma((2,)), dma((2,)), dma((2,)),
            dma((NA,)), dma((NA,)), dma((NA,)), dma((NA,)),
        ],
        compiler_params=pltpu.CompilerParams(
            collective_id=0, has_side_effects=True, vmem_limit_bytes=60 * 2**20
        ),
    )(cycle_state, core_t, core_taps.T, core_weights.T, cycle_taps.T, cycle_weights.T, tab, trig)
    return cycle_new, jnp.transpose(core_new, (0, 2, 1, 3))


def solution(mesh):
    placed = (P(None, "axial", "azim", None), P(None, "axial", "azim", None), P(), P(), P(), P())
    return jax.shard_map(
        body,
        mesh=mesh,
        in_specs=placed,
        out_specs=(P(None, "axial", "azim", None), P(None, "axial", "azim", None)),
        check_vma=False,
    )
```

time: 210 us -> 42.5 us (0.20)
  other arithmetic: 60.7 us -> 0 us
  waiting for transfers between devices: 36.8 us -> 0 us
  Pallas kernels: 0 us -> 35 us
  matrix products: 27.9 us -> 0 us
  local copies, waits for them, and re-layouts: 31.5 us -> 6.27 us
  blocking collectives: 22.2 us -> 0 us
  starting transfers between devices: 15.5 us -> 0 us
  between operations: 14.7 us -> 0.65 us
    reduce_scatter x1 -> x0, waiting for transfers between devices: 36.8 us -> none  [body(): lax.psum_scatter(cycle_share, 'azim', scatter_dimension=2, tiled=True)]
    pallas_call x0 -> x1, Pallas kernels: none -> 35 us  [body(): pl.pallas_call(kernel, out_shape=(jax.ShapeDtypeStruct(cycle_state.shape,...]
    dot_general x2 -> x0, matrix products: 27.9 us -> none  [apply_taps(): jnp.dot(flat_values, matrix, preferred_element_type=jnp.float32, precisio...]
    add x3 -> x0, other arithmetic: 26.4 us -> none  [the longest x1 25.6 us: body(): cycle_state + time_step * cycle_rhs(padded, inner_ghost, angle_step)]
    all_gather x1 -> x0, blocking collectives: 22.2 us -> none  [body(): all_traces = lax.all_gather(cart_trace, 'azim', axis=2, tiled=True)]
    unnamed x79 -> x4, local copies, waits for them, and re-layouts: 22.5 us -> 6.27 us
    ppermute x8 -> x0, starting transfers between devices: 15.5 us -> none  [the longest x4 13.8 us: padded_2(): lax.ppermute(lax.slice_in_dim(block, 0, width, axis=dim), axis, backward)]
    unnamed x22 -> x0, other arithmetic: 9.48 us -> none
  transfers between devices with their start and end apart: 9 -> 0, of which waited for: 1 -> 0; matrix products, arithmetic and copies ran while one was open for 27% -> 0% of each run, Pallas kernels for 0% -> 0%
where the time goes in v1:
time: 42.5 us; the launch traced here: 41.9 us
  Pallas kernels  35 us (82%)
  local copies, waits for them, and re-layouts  6.27 us (15%)
  between operations  0.65 us (2%)
    pallas_call x1, Pallas kernels, body(): pl.pallas_call(kernel, out_shape=(jax.ShapeDtypeStruct(cycle_state.shape,...  35 us
    unnamed x4, local copies, waits for them, and re-layouts  6.27 us

profile of v1, /device:TPU:0, one launch (start us, length us, event | category | flops | bytes accessed | tf_op | source)
XLA Modules:
  0.0 41.9 jit_solution(7177625087589897400)
XLA Ops:
  0.6 35.0 %shard_map.95 = (f32[5,8,128,256]{3,2,1,0:T(8,128)}, f32[5,12,8,192]{3,2,1,0:T(8,128)}) custom-call(f32[5,8,128,256]{3,2,1,0:T(8,128)} %cyc.1, f32[5,12,8,192]{3,2,1,0:T(8,128)} %bitcast.6, s32[4,768]{1,0:T(4,128)} %bitcast.10, f32[4,768]{1,0:T(4,128)} %bitcast.11, s32[4,2048]{1,0:T(4,128)} %bitcast.8, f32[4,2048]{1,0:T(4,128)} %bitcast.9, ...), custom_call_target="tpu_custom_call" | custom-call | tf_op jit(solution)/shard_map/pallas_call | solution.py:592
  35.7 0.0 copy-start
  35.7 5.5 %copy.12 = f32[5,8,128,256]{3,2,1,0:T(8,128)} copy(f32[5,8,128,256]{3,2,1,0:T(8,128)} %get-tuple-element.8) | data formatting | bytes 10485760
  41.2 0.0 copy-done
  41.2 0.8 %copy.13 = f32[5,8,12,192]{3,1,2,0:T(8,128)} copy(f32[5,8,12,192]{3,1,2,0:T(8,128)S(1)} %bitcast.7) | data formatting | bytes 737280
Async XLA Ops:
  35.7 5.5 %copy-start = (f32[5,12,8,192]{3,2,1,0:T(8,128)S(1)}, f32[5,12,8,192]{3,2,1,0:T(8,128)}, u32[]{:S(2)}) copy-start(f32[5,12,8,192]{3,2,1,0:T(8,128)} %get-tuple-element.5) | copy-start | bytes 1105924

commit v2 on v1

v2 whole, which is shorter than its diff:
```python
import functools
import math

import jax
import jax.numpy as jnp
import numpy as np
from jax import lax
from jax.experimental import pallas as pl
from jax.experimental.pallas import tpu as pltpu
from jax.sharding import PartitionSpec as P

DT = 0.001
DX = 0.004
DR = 1.0 / 256.0
DC = 2.0 / 192.0
NU = 0.002
NT = 2048
NR = 256
NC = 192
PL = 8
SEC = 128
ROWS = 12
W = 16
NA = 16
DA = 2.0 * math.pi / NT

BX = NU * DT / DX**2
AX = DT / (2.0 * DX)
BR = NU * DT / DR**2 / BX
AC = DT / (2.0 * DC) / BX
BC = NU * DT / DC**2 / BX
SX = DX / (2.0 * NU)


def tables():
    radius = lambda i: 1.0 + (i + 0.5) / 256.0
    i = np.arange(NR, dtype=np.float64)
    tab = np.zeros((8, NR))
    tab[0] = DT / (2.0 * DA * radius(i)) / BX
    tab[1] = NU * DT / (DA * radius(i)) ** 2 / BX
    tab[2] = DT * radius(i) / (2.0 * DR * radius(i - 1)) / BX
    tab[3] = DT * radius(i) / (2.0 * DR * radius(i + 1)) / BX
    tab[3, -1] = DT * radius(NR) / (2.0 * DR * radius(NR - 1)) / BX
    tab[4] = 1.0 / BX - 2.0 - 2.0 * BR - 2.0 * tab[1]
    tab[5] = DT / radius(i) / BX
    angle = (np.arange(NT) + 0.5) * (2.0 * math.pi / NT)
    trig = np.zeros((8, NT))
    trig[0] = np.cos(angle)
    trig[1] = np.sin(angle)
    return tab.astype(np.float32), trig.astype(np.float32)


INNER = float(DT * (1.0 - 0.5 / 256.0) / (2.0 * DR * (1.0 + 0.5 / 256.0)) / BX)
CC = float(1.0 / BX - 2.0 - 4.0 * BC)


def needed(a):
    found = set()
    for off in (0, 512):
        found |= {((32 * a - 8 + off) // SEC) % NA, ((32 * a + 37 + off) // SEC) % NA}
    if a == 0:
        found |= set(range(7, 13))
    if a == NA - 1:
        found |= {11, 12, 13, 14, 15, 0}
    return sorted(found)


def fluxes(q):
    inv = pltpu.reciprocal(q[0], approx=False)
    u1, u2, u3 = q[1] * inv, q[2] * inv, q[3] * inv
    p11, p22, p33 = q[1] * u1, q[2] * u2, q[3] * u3
    p12, p13, p23 = q[1] * u2, q[1] * u3, q[2] * u3
    pr = 0.4 * q[4] - 0.2 * (p11 + p22 + p33)
    h = q[4] + pr
    return (
        None,
        [q[1], p11 + pr, p12, p13, h * u1],
        [q[2], p12, p22 + pr, p23, h * u2],
        [q[3], p13, p23, p33 + pr, h * u3],
    )


def kernel(
    cyc, cor, ctaps, cwts, ytaps, ywts, tab_in, trig_in, ov, hal, ah, fix, cres, tab,
    qv, p2s, m2s, cin, cv, oc, chx, crlo, crhi, trs, trr, shs, shr, xm, ep, gl, gr, trig, ct, cw, yt, yw,
    in_sem, sm_sem, ax_s, ax_r, cx_s, cx_r, ar_s, ar_r, cr_s, cr_r, tr_s, tr_r, sh_s, sh_r,
):
    me = lax.axis_index("azim")
    ax = lax.axis_index("axial")
    n_ax = lax.axis_size("axial")
    up_ax = {"axial": lax.rem(ax + 1, n_ax)}
    dn_ax = {"axial": lax.rem(ax + n_ax - 1, n_ax)}
    up_az = {"azim": lax.rem(me + 1, NA)}
    dn_az = {"azim": lax.rem(me + NA - 1, NA)}
    MESH = pl.DeviceIdType.MESH

    barrier = pltpu.get_barrier_semaphore()
    pl.semaphore_signal(barrier, inc=1, device_id=up_ax, device_id_type=MESH)
    pl.semaphore_signal(barrier, inc=1, device_id=dn_ax, device_id_type=MESH)

    def greet(d, _):
        @pl.when(d != me)
        def _():
            pl.semaphore_signal(barrier, inc=1, device_id={"azim": d}, device_id_type=MESH)

        return 0

    lax.fori_loop(0, NA, greet, 0)

    smalls = [
        pltpu.make_async_copy(s, d, sm_sem.at[i])
        for i, (s, d) in enumerate(
            [(cor, cin), (ytaps, yt), (ywts, yw), (tab_in, tab), (trig_in, trig), (ctaps, ct), (cwts, cw)]
        )
    ]
    planes = [pltpu.make_async_copy(cyc.at[:, p], qv.at[:, p], in_sem.at[p]) for p in range(PL)]
    for c in smalls:
        c.start()
    for c in planes:
        c.start()

    def remote(src, dst, s, r, dev):
        return pltpu.make_async_remote_copy(
            src_ref=src, dst_ref=dst, send_sem=s, recv_sem=r, device_id=dev, device_id_type=MESH
        )

    axial = [
        remote(cyc.at[:, 0], hal.at[:, 1], ax_s.at[0], ax_r.at[0], dn_ax),
        remote(cyc.at[:, PL - 1], hal.at[:, 0], ax_s.at[1], ax_r.at[1], up_ax),
    ]
    caxial = [
        remote(cor.at[:, :, 0, :], chx.at[:, :, PL - 1, :], cx_s.at[0], cx_r.at[0], dn_ax),
        remote(cor.at[:, :, PL - 1, :], chx.at[:, :, 0, :], cx_s.at[1], cx_r.at[1], up_ax),
    ]
    azim = [
        remote(cyc.at[:, :, 0, :], ah.at[:, :, 7, :], ar_s.at[0], ar_r.at[0], dn_az),
        remote(cyc.at[:, :, SEC - 1, :], ah.at[:, :, 0, :], ar_s.at[1], ar_r.at[1], up_az),
    ]
    crow_dn = remote(cor.at[:, 0], crhi, cr_s.at[0], cr_r.at[0], dn_az)
    crow_up = remote(cor.at[:, ROWS - 1], crlo, cr_s.at[1], cr_r.at[1], up_az)

    lane8 = lax.broadcasted_iota(jnp.int32, (8, 128), 1)
    row8 = lax.broadcasted_iota(jnp.int32, (8, 128), 0)

    for c in smalls:
        c.wait()
    for i in range(ROWS):
        for c in range(5):
            cv[c, i + 1, :, 0:128] = cin[c, i, :, 0:128]
            cv[c, i + 1, :, 128:192] = cin[c, i, :, 128:192]

    for c in range(5):
        v = jnp.zeros((8, 128), jnp.float32)
        for i in range(ROWS):
            left = pltpu.roll(cv[c, i + 1, :, 0:128], 8 * i, 1)
            right = pltpu.roll(cv[c, i + 1, :, 128:256], (8 * i + 4 - 60) % 128, 1)
            v = jnp.where((lane8 >> 3) == i, jnp.where((lane8 & 7) < 4, left, right), v)
        ep[c, 6] = v

    def bcast(x):
        return jnp.broadcast_to(x, (8, 128))

    def tap_cells(d):
        cols = pl.ds(pl.multiple_of(d * SEC, SEC), SEC)
        ws = [yw[k : k + 1, cols] for k in range(4)]
        total = ws[0] + ws[1] + ws[2] + ws[3]
        cells = []
        for k in range(4):
            tap = bcast(yt[k : k + 1, cols])
            row = ((tap >> 6) * 43691) >> 17
            cells.append((row - me * ROWS, tap - row * NC, bcast(ws[k] / total)))
        return cells

    def share(d, _):
        acc = [jnp.zeros((8, 128), jnp.float32) for _ in range(5)]
        for lrow, col, w in tap_cells(d):
            inside = jnp.logical_and(lrow >= 0, lrow < ROWS)
            side = jnp.logical_or(col < 4, col >= NC - 4)
            idx = (lrow * 8 + jnp.where(col < 4, col, col - (NC - 8))) & 127
            wk = jnp.where(jnp.logical_and(inside, side), w, 0.0)
            for c in range(5):
                acc[c] = acc[c] + wk * jnp.take_along_axis(ep[c, 6], idx, axis=1)
        for c in range(5):
            shs[d, c] = acc[c]
        return 0

    lax.fori_loop(0, NA, share, 0, unroll=4)

    pl.semaphore_wait(barrier, NA - 1 + 2)
    for c in axial:
        c.start()
    for c in azim + caxial:
        c.start()

    @pl.when(me > 0)
    def _():
        crow_dn.start()

    @pl.when(me < NA - 1)
    def _():
        crow_up.start()

    @pl.when(jnp.logical_or(me == 0, me == NA - 1))
    def _():
        r0 = jnp.where(me == 0, 0, ROWS - 4)
        for c in range(5):
            for r in range(4):
                ep[c, r] = cv[c, r0 + r + 1, :, 0:128]
            for j in range(2):
                even = cv[c, r0 + 2 * j + 1, :, 128:256]
                odd = cv[c, r0 + 2 * j + 2, :, 128:256]
                ep[c, 4 + j] = jnp.where(lane8 < 64, even, pltpu.roll(odd, 64, 1))

        def outer(d, _):
            acc = [shs[d, c] for c in range(5)]
            for lrow, col, w in tap_cells(d):
                r = lrow - r0
                mid = jnp.logical_and(col >= 4, col < NC - 4)
                ok = jnp.logical_and(mid, jnp.logical_and(r >= 0, r < 4))
                wk = jnp.where(ok, w, 0.0)
                high = col >= 128
                group = jnp.where(high, 4 + (r >> 1), r)
                idx = jnp.where(high, (col & 63) + ((r & 1) << 6), col) & 127
                for s in range(6):
                    ws = jnp.where(group == s, wk, 0.0)
                    for c in range(5):
                        acc[c] = acc[c] + ws * jnp.take_along_axis(ep[c, s], idx, axis=1)
            for c in range(5):
                shs[d, c] = acc[c]
            return 0

        lax.fori_loop(0, NA, outer, 0, unroll=2)

    def sh_copy(d):
        return remote(shs.at[d], shr.at[me], sh_s.at[d], sh_r.at[me], {"azim": d})

    def send_share(d, _):
        @pl.when(d != me)
        def _():
            sh_copy(d).start()

        return 0

    lax.fori_loop(0, NA, send_share, 0)
    for c in range(5):
        shr[me, c] = shs[me, c]

    for c in planes:
        c.wait()

    lane_s = lax.broadcasted_iota(jnp.int32, (SEC, 128), 1)

    tt = jnp.zeros((SEC, 128), jnp.float32)
    for p in range(PL):
        for c in range(5):
            ch = c * 8 + p
            x = qv[c, p, :, 0:128]
            tt = jnp.where(lane_s == ch, pltpu.roll(x, ch, 1) if ch else x, tt)
    tt = tt.T
    own = pl.ds(pl.multiple_of(me * SEC, SEC), SEC)
    cosine = jnp.broadcast_to(trig[0:1, own], (8, 128))
    sine = jnp.broadcast_to(trig[1:2, own], (8, 128))
    tq = [tt[8 * c : 8 * c + 8, :] for c in range(5)]
    cart = [tq[0], tq[1], tq[3] * cosine - tq[2] * sine, tq[3] * sine + tq[2] * cosine, tq[4]]
    for c in range(5):
        trs[c] = cart[c]
        trr[me, c] = cart[c]

    def tr_copy(d):
        return remote(trs, trr.at[me], tr_s.at[d], tr_r.at[me], {"azim": d})

    def is_in(x, items):
        hit = x == items[0]
        for it in items[1:]:
            hit = jnp.logical_or(hit, x == it)
        return hit

    for a in range(NA):
        others = [s for s in needed(a) if s != a]

        @pl.when(is_in(me, others))
        def _(a=a):
            tr_copy(a).start()

    first, last = lane8 == 0, lane8 == 127
    zero8 = jnp.zeros((8, 128), jnp.float32)
    wide_first = lax.broadcasted_iota(jnp.int32, (W, 128), 1) == 0
    wide_last = lax.broadcasted_iota(jnp.int32, (W, 128), 1) == 127
    for c in range(5):
        for h in range(2):
            m2s[c, h, 2 * W - 8 : 2 * W, :] = zero8
            p2s[c, h, 2 * W + SEC : 2 * W + SEC + 8, :] = zero8
        ov[c, 1, W : W + SEC, :] = jnp.zeros((SEC, NR), jnp.float32)

    def cycle_plane(p, _):
        for b in range(SEC // W + 1):
            rows, prev, now = pl.ds(W * b + W, W), pl.ds(W * b, W), pl.ds(W * b + 2 * W, W)
            if b < SEC // W:
                q = [qv[c, p, W * b : W * b + W, :] for c in range(5)]
                _, f1, f2, f3 = fluxes(q)
                row = lambda k: jnp.broadcast_to(tab[k : k + 1, :], (W, NR))
                ka, ba, cp, cm, cc, so = [row(k) for k in range(6)]
                for c in range(5):
                    ov[c, p, rows, :] += q[c] - f1[c]
                    acc = ov[c, p + 1, rows, :] + cc * q[c]
                    ov[c, p + 2, rows, :] = q[c] + f1[c]
                    base = BR * q[c]
                    p3 = base - cp * f3[c]
                    m3 = base + cm * f3[c]
                    pl0, pl1 = pltpu.roll(p3[:, :128], 127, 1), pltpu.roll(p3[:, 128:], 127, 1)
                    ml0, ml1 = pltpu.roll(m3[:, :128], 1, 1), pltpu.roll(m3[:, 128:], 1, 1)
                    wall = m3[:, 128:] if c != 3 else -m3[:, 128:]
                    lo = jnp.where(wide_last, pl1, pl0) + jnp.where(wide_first, 0.0, ml0)
                    hi = jnp.where(wide_last, wall, pl1) + jnp.where(wide_first, ml0, ml1)
                    acc = acc + jnp.concatenate([lo, hi], axis=1)
                    if c == 2:
                        acc = acc - so * f2[3]
                    if c == 3:
                        acc = acc + so * f2[2]
                    ov[c, p + 1, rows, :] = acc
                    bq, kf = ba * q[c], ka * f2[c]
                    p2, m2 = bq - kf, bq + kf
                    for h in range(2):
                        half = slice(128 * h, 128 * h + 128)
                        p2s[c, h, now, :] = p2[:, half]
                        m2s[c, h, now, :] = m2[:, half]
            if b:
                for c in range(5):
                    for h in range(2):
                        half = slice(128 * h, 128 * h + 128)
                        up = p2s[c, h, pl.ds(W * b + W + 1, W), :]
                        dn = m2s[c, h, pl.ds(W * b + W - 1, W), :]
                        ov[c, p + 1, prev, half] += up + dn
        return 0

    lax.fori_loop(0, PL, cycle_plane, 0)

    for s in range(NA):
        takers = [a for a in range(NA) if s in needed(a) and a != s]

        @pl.when(is_in(me, takers))
        def _(s=s):
            remote(trs, trr.at[s], tr_s.at[s], tr_r.at[s], {"azim": s}).wait_recv()

    s0 = ((32 * me + 2040) >> 7) & 15
    s1 = ((32 * me + 37) >> 7) & 15

    def ghost(start, shift, sectors):
        vals = [zero8 for _ in range(5)]
        ws = [bcast_roll(cw[k : k + 1, start : start + 256], shift) for k in range(4)]
        total = ws[0] + ws[1] + ws[2] + ws[3]
        for k in range(4):
            tap = bcast_roll(ct[k : k + 1, start : start + 256], shift)
            idx = tap & 127
            sec = tap >> 7
            w = ws[k] / total
            for c in range(5):
                v = jnp.take_along_axis(trr[sectors[0], c], idx, axis=1)
                for s in sectors[1:]:
                    v = jnp.where(sec == s, jnp.take_along_axis(trr[s, c], idx, axis=1), v)
                vals[c] = vals[c] + w * v
        return vals

    def bcast_roll(x, shift):
        full = jnp.broadcast_to(x, (8, 256))
        if isinstance(shift, int):
            return full[:, shift : shift + 128]
        return pltpu.roll(full, shift, 1)[:, :128]

    def col_terms(g):
        return fluxes(g)[3]

    back = lax.rem(512 - ROWS * me, 256)
    g = ghost(0, back, [s0, s1])
    f = col_terms(g)
    for c in range(5):
        gl[c] = BC * g[c] + AC * f[c]
    back = lax.rem(512 - 64 - ROWS * me, 256)
    g = ghost(128, back, [(s0 + 4) & 15, (s1 + 4) & 15])
    f = col_terms(g)
    for c in range(5):
        gr[c] = BC * g[c] - AC * f[c]

    @pl.when(me > 0)
    def _():
        crow_up.wait_recv()
        for c in range(5):
            cv[c, 0, :, 0:128] = crlo[c, :, 0:128]
            cv[c, 0, :, 128:192] = crlo[c, :, 128:192]

    @pl.when(me < NA - 1)
    def _():
        crow_dn.wait_recv()
        for c in range(5):
            cv[c, ROWS + 1, :, 0:128] = crhi[c, :, 0:128]
            cv[c, ROWS + 1, :, 128:192] = crhi[c, :, 128:192]

    @pl.when(me == 0)
    def _():
        for h in range(2):
            g = ghost(384, 0, list(range(7, 13))) if h == 0 else ghost(384, 128, list(range(7, 13)))
            for c in range(5):
                cv[c, 0, :, 128 * h : 128 * h + 128] = g[c]

    @pl.when(me == NA - 1)
    def _():
        g = ghost(512, 64, [11, 12, 13, 14, 15, 0])
        for c in range(5):
            cv[c, ROWS + 1, :, 0:128] = g[c]
        g = ghost(512, 128, [11, 12, 13, 14, 15, 0])
        for c in range(5):
            cv[c, ROWS + 1, :, 128:256] = pltpu.roll(g[c], 64, 1)

    for c in caxial:
        c.wait_recv()

    sub = lax.broadcasted_iota(jnp.int32, (8, 256), 0)
    q = [cv[c, 0, :, :] for c in range(5)]
    f2 = fluxes(q)[2]
    for c in range(5):
        oc[c, 1] = BC * q[c] + AC * f2[c]
    for i in range(1, ROWS + 1):
        q = [cv[c, i, :, :] for c in range(5)]
        _, f1, f2, f3 = fluxes(q)
        x = [chx[c, i - 1, :, :] for c in range(5)]
        x = [jnp.concatenate([v, jnp.ones((8, 64), jnp.float32)], axis=1) for v in x]
        xf = fluxes(x)[1]
        for c in range(5):
            m1 = pltpu.roll(q[c] + f1[c], 1, 0)
            p1 = pltpu.roll(q[c] - f1[c], 7, 0)
            m1 = jnp.where(sub == 0, x[c] + xf[c], m1)
            p1 = jnp.where(sub == 7, x[c] - xf[c], p1)
            acc = oc[c, i] + CC * q[c] + m1 + p1
            base = BC * q[c]
            p3, m3 = base - AC * f3[c], base + AC * f3[c]
            a, bb = pltpu.roll(p3[:, :128], 127, 1), pltpu.roll(p3[:, 128:], 127, 1)
            e, f = pltpu.roll(m3[:, :128], 1, 1), pltpu.roll(m3[:, 128:], 1, 1)
            lg = pltpu.roll(gl[c], 129 - i, 1) if i > 1 else gl[c]
            rg = pltpu.roll(gr[c], 64 - i, 1)
            lo = jnp.where(last, bb, a) + jnp.where(first, lg, e)
            hi = jnp.where(lane8 == 63, rg, bb) + jnp.where(first, e, f)
            acc = acc + jnp.concatenate([lo, hi], axis=1)
            p2, m2 = base - AC * f2[c], base + AC * f2[c]
            if i > 1:
                done = BX * (oc[c, i - 1] + p2)
                cres[c, i - 2, :, 0:128] = done[:, 0:128]
                cres[c, i - 2, :, 128:192] = done[:, 128:192]
            oc[c, i] = acc
            if i < ROWS:
                oc[c, i + 1] = m2
    q = [cv[c, ROWS + 1, :, :] for c in range(5)]
    f2 = fluxes(q)[2]
    for c in range(5):
        done = BX * (oc[c, ROWS] + BC * q[c] - AC * f2[c])
        cres[c, ROWS - 1, :, 0:128] = done[:, 0:128]
        cres[c, ROWS - 1, :, 128:192] = done[:, 128:192]

    def await_share(d, _):
        @pl.when(d != me)
        def _():
            remote(shs.at[d], shr.at[d], sh_s.at[d], sh_r.at[d], {"azim": d}).wait_recv()

        return 0

    lax.fori_loop(0, NA, await_share, 0)
    cart = [functools.reduce(jnp.add, [shr[d, c] for d in range(NA)]) for c in range(5)]
    g = [cart[0], cart[1], cart[3] * cosine - cart[2] * sine, cart[2] * cosine + cart[3] * sine, cart[4]]
    f3 = fluxes(g)[3]
    for c in range(5):
        xm[8 * c : 8 * c + 8, :] = BR * g[c] + INNER * f3[c]
    fix[...] = xm[...].T
    for c in azim + axial:
        c.wait_recv()

    for c in axial + azim + caxial:
        c.wait_send()

    @pl.when(me > 0)
    def _():
        crow_dn.wait_send()

    @pl.when(me < NA - 1)
    def _():
        crow_up.wait_send()

    for a in range(NA):
        others = [s for s in needed(a) if s != a]

        @pl.when(is_in(me, others))
        def _(a=a):
            tr_copy(a).wait_send()

    def drain(d, _):
        @pl.when(d != me)
        def _():
            sh_copy(d).wait_send()

        return 0

    lax.fori_loop(0, NA, drain, 0)


def closing(ov, hal, ah, fix, core, tab, cyc_out, cor_out, buf, sems):
    core_copy = pltpu.make_async_copy(core, cor_out, sems.at[PL])
    core_copy.start()
    top = lax.broadcasted_iota(jnp.int32, (8, NR), 0) == 0
    bottom = lax.broadcasted_iota(jnp.int32, (8, NR), 0) == 7
    first = lax.broadcasted_iota(jnp.int32, (W, 128), 1) == 0
    ka = jnp.broadcast_to(tab[0:1, :], (8, NR))
    ba = jnp.broadcast_to(tab[1:2, :], (8, NR))

    def copy(p):
        return pltpu.make_async_copy(buf.at[:, p], cyc_out.at[:, p], sems.at[p])

    def plane(p, axial):
        side = [ah[c, p, :, :] for c in range(5)]
        f2 = fluxes(side)[2]
        lo = [jnp.where(top, ba * side[c] + ka * f2[c], 0.0) for c in range(5)]
        hi = [jnp.where(bottom, ba * side[c] - ka * f2[c], 0.0) for c in range(5)]
        for b in range(SEC // W):
            rows = slice(W * b, W * b + W)
            if axial is not None:
                q = [hal[c, axial, rows, :] for c in range(5)]
                f1 = fluxes(q)[1]
            inner = fix[rows, :]
            for c in range(5):
                v = ov[c, p + 1, W * b + W : W * b + 2 * W, :]
                if axial == 0:
                    v = v + (q[c] + f1[c])
                if axial == 1:
                    v = v + (q[c] - f1[c])
                if b == 0:
                    v = jnp.concatenate([v[:8] + lo[c], v[8:]], axis=0)
                if b == SEC // W - 1:
                    v = jnp.concatenate([v[: W - 8], v[W - 8 :] + hi[c]], axis=0)
                col = jnp.where(first, pltpu.roll(inner, lax.rem(128 - 8 * c - p, 128), 1), 0.0)
                buf[c, p, rows, 0:128] = BX * (v[:, :128] + col)
                buf[c, p, rows, 128:256] = BX * v[:, 128:]
        copy(p).start()

    def middle(p, _):
        plane(p, None)
        return 0

    lax.fori_loop(1, PL - 1, middle, 0)
    plane(jnp.int32(0), 0)
    plane(jnp.int32(PL - 1), 1)
    core_copy.wait()
    for p in range(PL):
        copy(p).wait()


def body(cycle_state, core_state, core_taps, core_weights, cycle_taps, cycle_weights):
    tab, trig = tables()
    f32, i32 = jnp.float32, jnp.int32
    dma = pltpu.SemaphoreType.DMA
    core_t = jnp.transpose(core_state, (0, 2, 1, 3))
    hbm = pl.BlockSpec(memory_space=pltpu.HBM)
    vmem = pl.BlockSpec(memory_space=pltpu.VMEM)
    vm = pltpu.VMEM
    shape = lambda *dims: jax.ShapeDtypeStruct(dims, f32)
    operands = [
        pltpu.with_memory_space_constraint(x, pltpu.HBM)
        for x in (
            cycle_state, core_t, core_taps.T, core_weights.T, cycle_taps.T, cycle_weights.T,
            jnp.asarray(tab), jnp.asarray(trig),
        )
    ]
    parts = pl.pallas_call(
        kernel,
        out_shape=(
            shape(5, PL + 2, SEC + W, NR),
            shape(5, 2, SEC, NR),
            shape(5, PL, 8, NR),
            shape(128, 128),
            shape(5, ROWS, PL, NC),
            shape(8, NR),
        ),
        in_specs=[hbm] * 8,
        out_specs=(vmem,) * 6,
        scratch_shapes=[
            vm((5, PL, SEC, NR), f32),
            vm((5, 2, SEC + 4 * W, 128), f32),
            vm((5, 2, SEC + 4 * W, 128), f32),
            vm((5, ROWS, PL, NC), f32),
            vm((5, ROWS + 2, PL, 256), f32),
            vm((5, ROWS + 2, PL, 256), f32),
            vm((5, ROWS, PL, NC), f32),
            vm((5, PL, NC), f32),
            vm((5, PL, NC), f32),
            vm((5, 8, 128), f32),
            vm((NA, 5, 8, 128), f32),
            vm((NA, 5, 8, 128), f32),
            vm((NA, 5, 8, 128), f32),
            vm((128, 128), f32),
            vm((5, 7, 8, 128), f32),
            vm((5, 8, 128), f32),
            vm((5, 8, 128), f32),
            vm((8, NT), f32),
            vm((4, 768), i32),
            vm((4, 768), f32),
            vm((4, NT), i32),
            vm((4, NT), f32),
            dma((PL,)),
            dma((7,)),
            dma((2,)), dma((2,)), dma((2,)), dma((2,)), dma((2,)), dma((2,)), dma((2,)), dma((2,)),
            dma((NA,)), dma((NA,)), dma((NA,)), dma((NA,)),
        ],
        compiler_params=pltpu.CompilerParams(
            collective_id=0, has_side_effects=True, vmem_limit_bytes=24 * 2**20
        ),
    )(*operands)
    cycle_new, core_new = pl.pallas_call(
        closing,
        out_shape=(
            jax.ShapeDtypeStruct(cycle_state.shape, f32),
            jax.ShapeDtypeStruct(core_t.shape, f32),
        ),
        in_specs=[vmem] * 6,
        out_specs=(hbm, hbm),
        scratch_shapes=[vm((5, PL, SEC, NR), f32), dma((PL + 1,))],
        compiler_params=pltpu.CompilerParams(vmem_limit_bytes=12 * 2**20),
    )(*parts)
    return cycle_new, jnp.transpose(core_new, (0, 2, 1, 3))


def solution(mesh):
    placed = (P(None, "axial", "azim", None), P(None, "axial", "azim", None), P(), P(), P(), P())
    return jax.shard_map(
        body,
        mesh=mesh,
        in_specs=placed,
        out_specs=(P(None, "axial", "azim", None), P(None, "axial", "azim", None)),
        check_vma=False,
    )
```

time: 42.5 us -> 23.9 us (0.56)
  the two profiles are of different devices: /device:TPU:0 before, /device:TPU:1 now
where the time goes in v2:
time: 23.9 us; the launch traced here: 23.8 us
  Pallas kernels  23.2 us (97%)
  between operations  0.64 us (3%)
    pallas_call x1, Pallas kernels, body(): pl.pallas_call(kernel, out_shape=(shape(5, PL + 2, SEC + W, NR), shape(5,...  20.6 us
    pallas_call x1, Pallas kernels, body(): pl.pallas_call(closing, out_shape=(jax.ShapeDtypeStruct(cycle_state.shape...  2.57 us

profile of v2, /device:TPU:1, one launch (start us, length us, event | category | flops | bytes accessed | tf_op | source)
XLA Modules:
  0.0 23.8 jit_solution(7829483871756270661)
XLA Ops:
  0.6 20.6 %shard_map.95 = (f32[5,10,144,256]{3,2,1,0:T(8,128)S(1)}, f32[5,2,128,256]{3,2,1,0:T(8,128)S(1)}, f32[5,8,8,256]{3,2,1,0:T(8,128)S(1)}, f32[128,128]{1,0:T(8,128...) custom-call(f32[5,8,128,256]{3,2,1,0:T(8,128)} %cyc.1, f32[5,12,8,192]{3,2,1,0:T(8,128)} %bitcast.6, ...), custom_call_target="tpu_custom_call" | custom-call | tf_op jit(solution)/shard_map/pallas_call | solution.py:569
  21.3 2.6 %shard_map.96 = (f32[5,8,128,256]{3,2,1,0:T(8,128)}, f32[5,12,8,192]{3,2,1,0:T(8,128)}) custom-call(f32[5,10,144,256]{3,2,1,0:T(8,128)S(1)} %get-tuple-element.10.ov, f32[5,2,128,256]{3,2,1,0:T(8,128)S(1)} %get-tuple-element.11.hal, f32[5,8,8,256]{3,2,1,0:T(8,128)S(1)} %get-tuple-element.12.ah, f32[128,128]{1,0:T(8,128)S(1)} %get-tuple-element.13.fix, ...), custom_call_target="tpu_custom_call" | custom-call | tf_op jit(solution)/shard_map/pallas_call | solution.py:613

commit v3 on v2

--- a/solution.py
+++ b/solution.py
@@ -22,6 +22,7 @@
 ROWS = 12
 W = 16
 NA = 16
+HUB = NA - 1
 DA = 2.0 * math.pi / NT
 
 BX = NU * DT / DX**2
@@ -83,7 +84,7 @@
 def kernel(
     cyc, cor, ctaps, cwts, ytaps, ywts, tab_in, trig_in, ov, hal, ah, fix, cres, tab,
     qv, p2s, m2s, cin, cv, oc, chx, crlo, crhi, trs, trr, shs, shr, xm, ep, gl, gr, trig, ct, cw, yt, yw,
-    in_sem, sm_sem, ax_s, ax_r, cx_s, cx_r, ar_s, ar_r, cr_s, cr_r, tr_s, tr_r, sh_s, sh_r,
+    all_in, in_sem, sm_sem, ax_s, ax_r, cx_s, cx_r, ar_s, ar_r, cr_s, cr_r, tr_s, tr_r, sh_s, sh_r,
 ):
     me = lax.axis_index("azim")
     ax = lax.axis_index("axial")
@@ -98,14 +99,15 @@
     pl.semaphore_signal(barrier, inc=1, device_id=up_ax, device_id_type=MESH)
     pl.semaphore_signal(barrier, inc=1, device_id=dn_ax, device_id_type=MESH)
 
+    @pl.when(jnp.logical_and(me != HUB, me != 0))
+    def _():
+        pl.semaphore_signal(barrier, inc=1, device_id={"azim": HUB}, device_id_type=MESH)
+
     def greet(d, _):
-        @pl.when(d != me)
-        def _():
-            pl.semaphore_signal(barrier, inc=1, device_id={"azim": d}, device_id_type=MESH)
-
-        return 0
-
-    lax.fori_loop(0, NA, greet, 0)
+        pl.semaphore_signal(barrier, inc=1, device_id={"azim": d}, device_id_type=MESH)
+        return 0
+
+    lax.fori_loop(1, jnp.where(me == 0, NA, 1), greet, 0)
 
     smalls = [
         pltpu.make_async_copy(s, d, sm_sem.at[i])
@@ -142,20 +144,39 @@
     lane8 = lax.broadcasted_iota(jnp.int32, (8, 128), 1)
     row8 = lax.broadcasted_iota(jnp.int32, (8, 128), 0)
 
-    for c in smalls:
-        c.wait()
-    for i in range(ROWS):
-        for c in range(5):
-            cv[c, i + 1, :, 0:128] = cin[c, i, :, 0:128]
-            cv[c, i + 1, :, 128:192] = cin[c, i, :, 128:192]
-
-    for c in range(5):
-        v = jnp.zeros((8, 128), jnp.float32)
+    def prepare():
+        for c in smalls:
+            c.wait()
         for i in range(ROWS):
-            left = pltpu.roll(cv[c, i + 1, :, 0:128], 8 * i, 1)
-            right = pltpu.roll(cv[c, i + 1, :, 128:256], (8 * i + 4 - 60) % 128, 1)
-            v = jnp.where((lane8 >> 3) == i, jnp.where((lane8 & 7) < 4, left, right), v)
-        ep[c, 6] = v
+            for c in range(5):
+                cv[c, i + 1, :, 0:128] = cin[c, i, :, 0:128]
+                cv[c, i + 1, :, 128:192] = cin[c, i, :, 128:192]
+
+        for c in range(5):
+            v = jnp.zeros((8, 128), jnp.float32)
+            for i in range(ROWS):
+                left = pltpu.roll(cv[c, i + 1, :, 0:128], 8 * i, 1)
+                right = pltpu.roll(cv[c, i + 1, :, 128:256], (8 * i + 4 - 60) % 128, 1)
+                v = jnp.where((lane8 >> 3) == i, jnp.where((lane8 & 7) < 4, left, right), v)
+            ep[c, 6] = v
+
+    @pl.when(ax < 2)
+    def _():
+        prepare()
+
+    pl.semaphore_wait(barrier, 2 + jnp.where(me == HUB, NA - 1, jnp.where(me == 0, 0, 1)))
+    for c in axial + caxial:
+        c.start()
+
+    def tell(d, _):
+        pl.semaphore_signal(all_in, inc=1, device_id={"azim": d}, device_id_type=MESH)
+        return 0
+
+    lax.fori_loop(0, jnp.where(me == HUB, NA - 1, 0), tell, 0)
+
+    @pl.when(ax >= 2)
+    def _():
+        prepare()
 
     def bcast(x):
         return jnp.broadcast_to(x, (8, 128))
@@ -186,23 +207,10 @@
 
     lax.fori_loop(0, NA, share, 0, unroll=4)
 
-    pl.semaphore_wait(barrier, NA - 1 + 2)
-    for c in axial:
-        c.start()
-    for c in azim + caxial:
-        c.start()
-
-    @pl.when(me > 0)
-    def _():
-        crow_dn.start()
-
-    @pl.when(me < NA - 1)
-    def _():
-        crow_up.start()
+    r0 = jnp.where(me == 0, 0, ROWS - 4)
 
     @pl.when(jnp.logical_or(me == 0, me == NA - 1))
     def _():
-        r0 = jnp.where(me == 0, 0, ROWS - 4)
         for c in range(5):
             for r in range(4):
                 ep[c, r] = cv[c, r0 + r + 1, :, 0:128]
@@ -211,25 +219,24 @@
                 odd = cv[c, r0 + 2 * j + 2, :, 128:256]
                 ep[c, 4 + j] = jnp.where(lane8 < 64, even, pltpu.roll(odd, 64, 1))
 
-        def outer(d, _):
-            acc = [shs[d, c] for c in range(5)]
-            for lrow, col, w in tap_cells(d):
-                r = lrow - r0
-                mid = jnp.logical_and(col >= 4, col < NC - 4)
-                ok = jnp.logical_and(mid, jnp.logical_and(r >= 0, r < 4))
-                wk = jnp.where(ok, w, 0.0)
-                high = col >= 128
-                group = jnp.where(high, 4 + (r >> 1), r)
-                idx = jnp.where(high, (col & 63) + ((r & 1) << 6), col) & 127
-                for s in range(6):
-                    ws = jnp.where(group == s, wk, 0.0)
-                    for c in range(5):
-                        acc[c] = acc[c] + ws * jnp.take_along_axis(ep[c, s], idx, axis=1)
-            for c in range(5):
-                shs[d, c] = acc[c]
-            return 0
-
-        lax.fori_loop(0, NA, outer, 0, unroll=2)
+    def outer(d, _):
+        acc = [shs[d, c] for c in range(5)]
+        for lrow, col, w in tap_cells(d):
+            r = lrow - r0
+            mid = jnp.logical_and(col >= 4, col < NC - 4)
+            ok = jnp.logical_and(mid, jnp.logical_and(r >= 0, r < 4))
+            wk = jnp.where(ok, w, 0.0)
+            high = col >= 128
+            group = jnp.where(high, 4 + (r >> 1), r)
+            idx = jnp.where(high, (col & 63) + ((r & 1) << 6), col) & 127
+            for s in range(6):
+                ws = jnp.where(group == s, wk, 0.0)
+                for c in range(5):
+                    acc[c] = acc[c] + ws * jnp.take_along_axis(ep[c, s], idx, axis=1)
+        for c in range(5):
+            shs[d, c] = acc[c]
+        return 0
+
 
     def sh_copy(d):
         return remote(shs.at[d], shr.at[me], sh_s.at[d], sh_r.at[me], {"azim": d})
@@ -241,46 +248,30 @@
 
         return 0
 
-    lax.fori_loop(0, NA, send_share, 0)
-    for c in range(5):
-        shr[me, c] = shs[me, c]
-
-    for c in planes:
-        c.wait()
+    def outer_and_send(d, _):
+        outer(d, 0)
+        return send_share(d, 0)
 
     lane_s = lax.broadcasted_iota(jnp.int32, (SEC, 128), 1)
-
-    tt = jnp.zeros((SEC, 128), jnp.float32)
-    for p in range(PL):
-        for c in range(5):
-            ch = c * 8 + p
-            x = qv[c, p, :, 0:128]
-            tt = jnp.where(lane_s == ch, pltpu.roll(x, ch, 1) if ch else x, tt)
-    tt = tt.T
     own = pl.ds(pl.multiple_of(me * SEC, SEC), SEC)
     cosine = jnp.broadcast_to(trig[0:1, own], (8, 128))
     sine = jnp.broadcast_to(trig[1:2, own], (8, 128))
-    tq = [tt[8 * c : 8 * c + 8, :] for c in range(5)]
-    cart = [tq[0], tq[1], tq[3] * cosine - tq[2] * sine, tq[3] * sine + tq[2] * cosine, tq[4]]
-    for c in range(5):
-        trs[c] = cart[c]
-        trr[me, c] = cart[c]
-
-    def tr_copy(d):
-        return remote(trs, trr.at[me], tr_s.at[d], tr_r.at[me], {"azim": d})
-
-    def is_in(x, items):
-        hit = x == items[0]
-        for it in items[1:]:
-            hit = jnp.logical_or(hit, x == it)
-        return hit
-
-    for a in range(NA):
-        others = [s for s in needed(a) if s != a]
-
-        @pl.when(is_in(me, others))
-        def _(a=a):
-            tr_copy(a).start()
+
+    def trace():
+        for c in planes:
+            c.wait()
+        tt = jnp.zeros((SEC, 128), jnp.float32)
+        for p in range(PL):
+            for c in range(5):
+                ch = c * 8 + p
+                x = qv[c, p, :, 0:128]
+                tt = jnp.where(lane_s == ch, pltpu.roll(x, ch, 1) if ch else x, tt)
+        tt = tt.T
+        tq = [tt[8 * c : 8 * c + 8, :] for c in range(5)]
+        cart = [tq[0], tq[1], tq[3] * cosine - tq[2] * sine, tq[3] * sine + tq[2] * cosine, tq[4]]
+        for c in range(5):
+            trs[c] = cart[c]
+            trr[me, c] = cart[c]
 
     first, last = lane8 == 0, lane8 == 127
     zero8 = jnp.zeros((8, 128), jnp.float32)
@@ -333,7 +324,68 @@
                         ov[c, p + 1, prev, half] += up + dn
         return 0
 
-    lax.fori_loop(0, PL, cycle_plane, 0)
+    ahead = jnp.where(me == 0, 0, jnp.maximum((12 - me) // 4, 0))
+    trace()
+
+    @pl.when(me == 0)
+    def _():
+        lax.fori_loop(0, NA, outer, 0, unroll=2)
+
+    def tr_copy(d):
+        return remote(trs, trr.at[me], tr_s.at[d], tr_r.at[me], {"azim": d})
+
+    def is_in(x, items):
+        hit = x == items[0]
+        for it in items[1:]:
+            hit = jnp.logical_or(hit, x == it)
+        return hit
+
+    between = jnp.logical_and(me != 0, me != HUB)
+
+    @pl.when(jnp.logical_and(between, is_in(me, [s for s in needed(0) if s])))
+    def _():
+        tr_copy(0).start()
+
+    @pl.when(between)
+    def _():
+        sh_copy(0).start()
+
+    lax.fori_loop(0, ahead, cycle_plane, 0)
+
+    @pl.when(me != HUB)
+    def _():
+        pl.semaphore_wait(all_in, 1)
+
+    for a in range(NA):
+        others = [s for s in needed(a) if s != a]
+
+        @pl.when(is_in(me, [HUB] if a == 0 else others))
+        def _(a=a):
+            tr_copy(a).start()
+
+    for c in azim:
+        c.start()
+
+    @pl.when(me > 0)
+    def _():
+        crow_dn.start()
+
+    @pl.when(me < NA - 1)
+    def _():
+        crow_up.start()
+
+    @pl.when(me == NA - 1)
+    def _():
+        lax.fori_loop(0, NA, outer_and_send, 0)
+
+    @pl.when(me != NA - 1)
+    def _():
+        lax.fori_loop(1, NA, send_share, 0)
+
+    for c in range(5):
+        shr[me, c] = shs[me, c]
+
+    lax.fori_loop(ahead, PL, cycle_plane, 0)
 
     for s in range(NA):
         takers = [a for a in range(NA) if s in needed(a) and a != s]
@@ -364,7 +416,7 @@
     def bcast_roll(x, shift):
         full = jnp.broadcast_to(x, (8, 256))
         if isinstance(shift, int):
-            return full[:, shift : shift + 128]
+            return (pltpu.roll(full, 256 - shift, 1) if shift else full)[:, :128]
         return pltpu.roll(full, shift, 1)[:, :128]
 
     def col_terms(g):
@@ -407,9 +459,9 @@
         g = ghost(512, 64, [11, 12, 13, 14, 15, 0])
         for c in range(5):
             cv[c, ROWS + 1, :, 0:128] = g[c]
-        g = ghost(512, 128, [11, 12, 13, 14, 15, 0])
-        for c in range(5):
-            cv[c, ROWS + 1, :, 128:256] = pltpu.roll(g[c], 64, 1)
+        g = ghost(512, 192, [11, 12, 13, 14, 15, 0])
+        for c in range(5):
+            cv[c, ROWS + 1, :, 128:256] = g[c]
 
     for c in caxial:
         c.wait_recv()
@@ -601,6 +653,7 @@
             vm((4, 768), f32),
             vm((4, NT), i32),
             vm((4, NT), f32),
+            pltpu.SemaphoreType.REGULAR,
             dma((PL,)),
             dma((7,)),
             dma((2,)), dma((2,)), dma((2,)), dma((2,)), dma((2,)), dma((2,)), dma((2,)), dma((2,)),

time: 23.9 us -> 21.7 us (0.908)
  the two profiles are of different devices: /device:TPU:1 before, /device:TPU:0 now
where the time goes in v3:
time: 21.7 us; the launch traced here: 21.6 us
  Pallas kernels  20.9 us (96%)
  between operations  0.64 us (3%)
    pallas_call x1, Pallas kernels, body(): pl.pallas_call(kernel, out_shape=(shape(5, PL + 2, SEC + W, NR), shape(5,...  18.3 us
    pallas_call x1, Pallas kernels, body(): pl.pallas_call(closing, out_shape=(jax.ShapeDtypeStruct(cycle_state.shape...  2.57 us

profile of v3, /device:TPU:0, one launch (start us, length us, event | category | flops | bytes accessed | tf_op | source)
XLA Modules:
  0.0 21.6 jit_solution(2456185717322134153)
XLA Ops:
  0.6 18.3 %shard_map.95 = (f32[5,10,144,256]{3,2,1,0:T(8,128)S(1)}, f32[5,2,128,256]{3,2,1,0:T(8,128)S(1)}, f32[5,8,8,256]{3,2,1,0:T(8,128)S(1)}, f32[128,128]{1,0:T(8,128...) custom-call(f32[5,8,128,256]{3,2,1,0:T(8,128)} %cyc.1, f32[5,12,8,192]{3,2,1,0:T(8,128)} %bitcast.6, ...), custom_call_target="tpu_custom_call" | custom-call | tf_op jit(solution)/shard_map/pallas_call | solution.py:621
  19.0 2.6 %shard_map.96 = (f32[5,8,128,256]{3,2,1,0:T(8,128)}, f32[5,12,8,192]{3,2,1,0:T(8,128)}) custom-call(f32[5,10,144,256]{3,2,1,0:T(8,128)S(1)} %get-tuple-element.10.ov, f32[5,2,128,256]{3,2,1,0:T(8,128)S(1)} %get-tuple-element.11.hal, f32[5,8,8,256]{3,2,1,0:T(8,128)S(1)} %get-tuple-element.12.ah, f32[128,128]{1,0:T(8,128)S(1)} %get-tuple-element.13.fix, ...), custom_call_target="tpu_custom_call" | custom-call | tf_op jit(solution)/shard_map/pallas_call | solution.py:666

commit v4 on v3

--- a/solution.py
+++ b/solution.py
@@ -56,14 +56,17 @@
 
 
 def needed(a):
-    found = set()
-    for off in (0, 512):
-        found |= {((32 * a - 8 + off) // SEC) % NA, ((32 * a + 37 + off) // SEC) % NA}
+    spans = [(32 * a - 8, 32 * a + 37), (32 * a + 504, 32 * a + 549)]
     if a == 0:
-        found |= set(range(7, 13))
+        spans.append((1016, 1541))
     if a == NA - 1:
-        found |= {11, 12, 13, 14, 15, 0}
-    return sorted(found)
+        spans.append((1528, 2053))
+    full, edge = set(), set()
+    for lo, hi in spans:
+        for s in range(lo // SEC, hi // SEC + 1):
+            start, stop = max(lo - s * SEC, 0), min(hi - s * SEC, SEC - 1)
+            (edge if stop < 8 or start >= SEC - 8 else full).add(s % NA)
+    return sorted(full - {a}), sorted(edge - full - {a})
 
 
 def fluxes(q):
@@ -83,7 +86,7 @@
 
 def kernel(
     cyc, cor, ctaps, cwts, ytaps, ywts, tab_in, trig_in, ov, hal, ah, fix, cres, tab,
-    qv, p2s, m2s, cin, cv, oc, chx, crlo, crhi, trs, trr, shs, shr, xm, ep, gl, gr, trig, ct, cw, yt, yw,
+    qv, p2s, m2s, cin, cv, oc, chx, crlo, crhi, trs, tre, trr, shs, shr, xm, ep, gl, gr, trig, ct, cw, yt, yw,
     all_in, in_sem, sm_sem, ax_s, ax_r, cx_s, cx_r, ar_s, ar_r, cr_s, cr_r, tr_s, tr_r, sh_s, sh_r,
 ):
     me = lax.axis_index("azim")
@@ -269,9 +272,14 @@
         tt = tt.T
         tq = [tt[8 * c : 8 * c + 8, :] for c in range(5)]
         cart = [tq[0], tq[1], tq[3] * cosine - tq[2] * sine, tq[3] * sine + tq[2] * cosine, tq[4]]
+        ends = jnp.zeros((8, 128), jnp.float32)
         for c in range(5):
             trs[c] = cart[c]
             trr[me, c] = cart[c]
+            head = pltpu.roll(cart[c], 16 * c, 1) if c else cart[c]
+            tail = pltpu.roll(cart[c], (16 * c + 16) % 128, 1)
+            ends = jnp.where((lane8 >> 4) == c, jnp.where((lane8 & 15) < 8, head, tail), ends)
+        trs[5] = ends
 
     first, last = lane8 == 0, lane8 == 127
     zero8 = jnp.zeros((8, 128), jnp.float32)
@@ -331,8 +339,10 @@
     def _():
         lax.fori_loop(0, NA, outer, 0, unroll=2)
 
-    def tr_copy(d):
-        return remote(trs, trr.at[me], tr_s.at[d], tr_r.at[me], {"azim": d})
+    def tr_copy(d, src, edge):
+        if edge:
+            return remote(trs.at[5], tre.at[src], tr_s.at[d], tr_r.at[src], {"azim": d})
+        return remote(trs.at[0:5], trr.at[src], tr_s.at[d], tr_r.at[src], {"azim": d})
 
     def is_in(x, items):
         hit = x == items[0]
@@ -342,9 +352,11 @@
 
     between = jnp.logical_and(me != 0, me != HUB)
 
-    @pl.when(jnp.logical_and(between, is_in(me, [s for s in needed(0) if s])))
-    def _():
-        tr_copy(0).start()
+    for edge in range(2):
+
+        @pl.when(jnp.logical_and(between, is_in(me, needed(0)[edge])))
+        def _(edge=edge):
+            tr_copy(0, me, edge).start()
 
     @pl.when(between)
     def _():
@@ -357,11 +369,13 @@
         pl.semaphore_wait(all_in, 1)
 
     for a in range(NA):
-        others = [s for s in needed(a) if s != a]
-
-        @pl.when(is_in(me, [HUB] if a == 0 else others))
-        def _(a=a):
-            tr_copy(a).start()
+        for edge in range(2):
+            givers = [s for s in needed(a)[edge] if a or s == HUB]
+            if givers:
+
+                @pl.when(is_in(me, givers))
+                def _(a=a, edge=edge):
+                    tr_copy(a, me, edge).start()
 
     for c in azim:
         c.start()
@@ -388,11 +402,19 @@
     lax.fori_loop(ahead, PL, cycle_plane, 0)
 
     for s in range(NA):
-        takers = [a for a in range(NA) if s in needed(a) and a != s]
-
-        @pl.when(is_in(me, takers))
-        def _(s=s):
-            remote(trs, trr.at[s], tr_s.at[s], tr_r.at[s], {"azim": s}).wait_recv()
+        for edge in range(2):
+            takers = [a for a in range(NA) if s in needed(a)[edge]]
+            if takers:
+
+                @pl.when(is_in(me, takers))
+                def _(s=s, edge=edge):
+                    tr_copy(s, s, edge).wait_recv()
+                    if edge:
+                        for c in range(5):
+                            ends = tre[s]
+                            head = pltpu.roll(ends, 128 - 16 * c, 1) if c else ends
+                            tail = pltpu.roll(ends, 112 - 16 * c, 1)
+                            trr[s, c] = jnp.where(lane8 < 8, head, tail)
 
     s0 = ((32 * me + 2040) >> 7) & 15
     s1 = ((32 * me + 37) >> 7) & 15
@@ -536,11 +558,13 @@
         crow_up.wait_send()
 
     for a in range(NA):
-        others = [s for s in needed(a) if s != a]
-
-        @pl.when(is_in(me, others))
-        def _(a=a):
-            tr_copy(a).wait_send()
+        for edge in range(2):
+            givers = needed(a)[edge]
+            if givers:
+
+                @pl.when(is_in(me, givers))
+                def _(a=a, edge=edge):
+                    tr_copy(a, me, edge).wait_send()
 
     def drain(d, _):
         @pl.when(d != me)
@@ -640,7 +664,8 @@
             vm((5, ROWS, PL, NC), f32),
             vm((5, PL, NC), f32),
             vm((5, PL, NC), f32),
-            vm((5, 8, 128), f32),
+            vm((6, 8, 128), f32),
+            vm((NA, 8, 128), f32),
             vm((NA, 5, 8, 128), f32),
             vm((NA, 5, 8, 128), f32),
             vm((NA, 5, 8, 128), f32),

time: 21.7 us -> 21.3 us (0.982)
  Pallas kernels: 20.9 us -> 20.6 us
    pallas_call x1, Pallas kernels: 18.3 us -> 18 us  [body(): pl.pallas_call(kernel, out_shape=(shape(5, PL + 2, SEC + W, NR), shape(5,...]
where the time goes in v4:
time: 21.3 us; the launch traced here: 21.2 us
  Pallas kernels  20.6 us (97%)
  between operations  0.64 us (3%)
    pallas_call x1, Pallas kernels, body(): pl.pallas_call(kernel, out_shape=(shape(5, PL + 2, SEC + W, NR), shape(5,...  18 us
    pallas_call x1, Pallas kernels, body(): pl.pallas_call(closing, out_shape=(jax.ShapeDtypeStruct(cycle_state.shape...  2.57 us

profile of v4, /device:TPU:0, one launch (start us, length us, event | category | flops | bytes accessed | tf_op | source)
XLA Modules:
  0.0 21.2 jit_solution(2280846015180415193)
XLA Ops:
  0.6 18.0 %shard_map.95 = (f32[5,10,144,256]{3,2,1,0:T(8,128)S(1)}, f32[5,2,128,256]{3,2,1,0:T(8,128)S(1)}, f32[5,8,8,256]{3,2,1,0:T(8,128)S(1)}, f32[128,128]{1,0:T(8,128...) custom-call(f32[5,8,128,256]{3,2,1,0:T(8,128)} %cyc.1, f32[5,12,8,192]{3,2,1,0:T(8,128)} %bitcast.6, ...), custom_call_target="tpu_custom_call" | custom-call | tf_op jit(solution)/shard_map/pallas_call | solution.py:645
  18.6 2.6 %shard_map.96 = (f32[5,8,128,256]{3,2,1,0:T(8,128)}, f32[5,12,8,192]{3,2,1,0:T(8,128)}) custom-call(f32[5,10,144,256]{3,2,1,0:T(8,128)S(1)} %get-tuple-element.10.ov, f32[5,2,128,256]{3,2,1,0:T(8,128)S(1)} %get-tuple-element.11.hal, f32[5,8,8,256]{3,2,1,0:T(8,128)S(1)} %get-tuple-element.12.ah, f32[128,128]{1,0:T(8,128)S(1)} %get-tuple-element.13.fix, ...), custom_call_target="tpu_custom_call" | custom-call | tf_op jit(solution)/shard_map/pallas_call | solution.py:691

commit v5 on v4

--- a/solution.py
+++ b/solution.py
@@ -250,6 +250,16 @@
             sh_copy(d).start()
 
         return 0
+
+    even = lax.rem(ax, 2) == 0
+
+    @pl.when(jnp.logical_and(even, me == HUB))
+    def _():
+        outer(0, 0)
+
+    @pl.when(jnp.logical_and(even, me != 0))
+    def _():
+        sh_copy(0).start()
 
     def outer_and_send(d, _):
         outer(d, 0)
@@ -358,7 +368,7 @@
         def _(edge=edge):
             tr_copy(0, me, edge).start()
 
-    @pl.when(between)
+    @pl.when(jnp.logical_and(between, jnp.logical_not(even)))
     def _():
         sh_copy(0).start()
 
@@ -390,7 +400,7 @@
 
     @pl.when(me == NA - 1)
     def _():
-        lax.fori_loop(0, NA, outer_and_send, 0)
+        lax.fori_loop(jnp.where(even, 1, 0), NA, outer_and_send, 0)
 
     @pl.when(me != NA - 1)
     def _():

time: 21.3 us -> 21.4 us (level)
  no operation moved by 1% of the time
where the time goes in v5:
time: 21.4 us; the launch traced here: 21.3 us
  Pallas kernels  20.7 us (97%)
  between operations  0.64 us (3%)
    pallas_call x1, Pallas kernels, body(): pl.pallas_call(kernel, out_shape=(shape(5, PL + 2, SEC + W, NR), shape(5,...  18.1 us
    pallas_call x1, Pallas kernels, body(): pl.pallas_call(closing, out_shape=(jax.ShapeDtypeStruct(cycle_state.shape...  2.57 us

profile of v5, /device:TPU:0, one launch (start us, length us, event | category | flops | bytes accessed | tf_op | source)
XLA Modules:
  0.0 21.3 jit_solution(5874446097774499762)
XLA Ops:
  0.6 18.1 %shard_map.95 = (f32[5,10,144,256]{3,2,1,0:T(8,128)S(1)}, f32[5,2,128,256]{3,2,1,0:T(8,128)S(1)}, f32[5,8,8,256]{3,2,1,0:T(8,128)S(1)}, f32[128,128]{1,0:T(8,128...) custom-call(f32[5,8,128,256]{3,2,1,0:T(8,128)} %cyc.1, f32[5,12,8,192]{3,2,1,0:T(8,128)} %bitcast.6, ...), custom_call_target="tpu_custom_call" | custom-call | tf_op jit(solution)/shard_map/pallas_call | solution.py:655
  18.8 2.6 %shard_map.96 = (f32[5,8,128,256]{3,2,1,0:T(8,128)}, f32[5,12,8,192]{3,2,1,0:T(8,128)}) custom-call(f32[5,10,144,256]{3,2,1,0:T(8,128)S(1)} %get-tuple-element.10.ov, f32[5,2,128,256]{3,2,1,0:T(8,128)S(1)} %get-tuple-element.11.hal, f32[5,8,8,256]{3,2,1,0:T(8,128)S(1)} %get-tuple-element.12.ah, f32[128,128]{1,0:T(8,128)S(1)} %get-tuple-element.13.fix, ...), custom_call_target="tpu_custom_call" | custom-call | tf_op jit(solution)/shard_map/pallas_call | solution.py:701
